TPU v7x, 1024 devices: a whole 4x4x32 slice. The times are simulated.
1024 devices in a mesh: dp: 256 (over x, z, core), col: 4 (over y).
Axes of the slice: x: 4, y: 4, z: 32, core: 2. Of those that a mesh axis runs over, the one named last changes fastest.
Arguments:
- queries: bfloat16 [1024, 2048], P('dp'), may hold values from -6 to 6
- kernel_inv: bfloat16 [2048, 2048], P(None, 'col'), may hold values from -0.125 to 0.125
- train_grads: bfloat16 [262144, 2048], P('dp'), may hold values from -0.125 to 0.125
- candidates: int32 [1024, 128], replicated, may hold values from 0 to 255, all different within a row
- block_slot: int32 [256], replicated, may hold values from 0 to 255, each once
Outputs:
- scores: bfloat16 [1024, 262144], P('col', 'dp')
Inputs may be any that keep to these rules, and one draw needn't show every extreme that they name: `candidates`: each row names 128 different blocks, and every block is named by some row. `block_slot`: each slot once.
All inputs are finite; a program needn't handle non-finite values.
Results may differ from a plain program's by a relative error of at most 0.0049.
Values may be sent and summed in bfloat16 or wider, within the bound.
A program may use at most 32 MiB of HBM per device.

v0:
```python
import jax
import jax.numpy as jnp
from jax import lax
from jax.sharding import PartitionSpec as P

B_DEV = 1


def listed_flags(candidates, block_slot, first_row, row_count, blocks_here, dp_index):
    owned_rows = lax.dynamic_slice_in_dim(candidates, first_row, row_count, 0)
    slot_ids = dp_index * blocks_here + jnp.arange(blocks_here, dtype=jnp.int32)
    numbers = jnp.arange(block_slot.shape[0], dtype=jnp.int32)
    owners = jnp.sum(
        jnp.where(block_slot[None, :] == slot_ids[:, None], numbers[None, :], 0), axis=1
    )
    flags = jnp.any(owned_rows[:, :, None] == owners[None, None, :], axis=1)
    return flags.astype(jnp.float32)


def per_device(queries, kernel_inv, train_grads, candidates, block_slot):
    n_col = lax.axis_size("col")
    col_index = lax.axis_index("col")
    dp_index = lax.axis_index("dp")
    total_queries = candidates.shape[0]
    per_col = total_queries // n_col
    first_row = col_index * per_col
    example_rows = train_grads.shape[0]
    block_rows = example_rows // B_DEV
    precond = jnp.dot(queries, kernel_inv, preferred_element_type=jnp.float32).astype(jnp.bfloat16)
    full_rows = lax.all_gather(precond, "col", axis=1, tiled=True)
    everyone = lax.all_gather(full_rows, "dp", axis=0, tiled=True)
    selected = lax.dynamic_slice_in_dim(everyone, first_row, per_col, 0)
    partial_scores = lax.dot_general(
        selected, train_grads, (((1,), (1,)), ((), ())), preferred_element_type=jnp.float32
    )
    flags = listed_flags(candidates, block_slot, first_row, per_col, B_DEV, dp_index)
    masked = partial_scores.reshape(per_col, B_DEV, block_rows) * flags[:, :, None]
    return masked.reshape(per_col, example_rows).astype(jnp.bfloat16)


def solution(mesh):
    placed = (P("dp", None), P(None, "col"), P("dp", None), P(), P())
    return jax.shard_map(
        per_device, mesh=mesh, in_specs=placed, out_specs=P("col", "dp"), check_vma=False
    )
```

profile of v0, /device:TPU:1, one launch (start us, length us, event | category | flops | bytes accessed | tf_op | source)
XLA Modules:
  0.0 316.4 jit_solution(12704827425163684202)
XLA Ops:
  6.5 0.0 copy-start
  6.5 0.0 all-gather.3.cloned.1.call-start
  6.5 1.6 copy-done
  8.1 1.1 convolution_convert_fusion
  9.2 11.0 %all_gather.6 = bf16[4,2048]{1,0:T(4,128)(2,1)} all-gather(bf16[4,512]{1,0:T(4,128)(2,1)S(1)} %convolution_convert_fusion), channel_id=1, replica_groups=mesh['dp'=256,'col'=4] {'col'}, dimensions={1}, use_global_device_ids=true | all-gather | bytes 20480 | tf_op jit(solution)/shard_map/all_gather | solution.py:30
  20.2 0.0 all-gather.3.cloned.1.call-update
  20.2 1.3 fusion.3
  21.5 1.7 fusion.2
  23.2 274.8 %all-gather.3.cloned.1.call-done = bf16[256,4,2048]{2,1,0:T(4,128)(2,1)} async-done(((bf16[1,4,2048]{2,1,0:T(4,128)(2,1)}), bf16[256,4,2048]{2,1,0:T(4,128)(2,1)}) %all-gather.3.cloned.1.call-update) | async-done | bytes 4194320 | tf_op jit(solution)/shard_map/all_gather | solution.py:31
  298.0 6.9 %reshape.26 = bf16[1024,2048]{1,0:T(8,128)(2,1)} reshape(bf16[256,4,2048]{2,1,0:T(4,128)(2,1)} %all-gather.3.cloned.1.call-done) | data formatting | bytes 8388608
  304.9 4.6 %fusion = bf16[256,1024]{1,0:T(8,128)(2,1)} fusion(bf16[1024,2048]{1,0:T(8,128)(2,1)} %param.7, bf16[1024,2048]{1,0:T(8,128)(2,1)} %reshape.26, s32[]{:T(128)S(6)} %select_n.9, f32[256]{0:T(256)S(1)} %convert_element_type.16), kind=kOutput, calls=%fused_computation.1 | convolution fusion | flops 1074266112 | bytes 5768196 | tf_op jit(solution)/shard_map/dot_general | solution.py:33
  (1 shorter events, 0.0 us)
Async XLA Ops:
  6.5 1.6 copy-start
  6.5 291.5 %all-gather.3.cloned.1.call-start = ((), (), s32[]{:S(2)}) async-start(), calls=%async_computation | async-start | bytes 4210688 | tf_op jit(solution)/shard_map/all_gather | solution.py:31
Sparse Core Ops, SparseCore 0:
  20.3 277.6 all-gather.2
where the time goes:
time: 317 us; the launch traced here: 316 us
  waiting for transfers between devices  275 us (87%)
  between operations  13.4 us (4%)
  blocking collectives  11 us (3%)
  local copies, waits for them, and re-layouts  8.48 us (3%)
  matrix products  5.68 us (2%)
    all_gather x1, waiting for transfers between devices, per_device(): everyone = lax.all_gather(full_rows, 'dp', axis=0, tiled=True)  275 us
    all_gather x1, blocking collectives, per_device(): full_rows = lax.all_gather(precond, 'col', axis=1, tiled=True)  11 us
    unnamed x3, local copies, waits for them, and re-layouts  8.48 us
  transfers between devices with their start and end apart: 1, of which 1 were waited for; matrix products, arithmetic and copies ran while one was open for 1% of the time, Pallas kernels for 0%

commit v1 on v0

v1 whole, which is shorter than its diff:
```python
import numpy as np
import jax
import jax.numpy as jnp
from jax import lax
from jax.sharding import Mesh, PartitionSpec as P


def listed_flags(candidates, block_slot, first_row, row_count, dp_index):
    owned_rows = lax.dynamic_slice_in_dim(candidates, first_row, row_count, 0)
    numbers = jnp.arange(block_slot.shape[0], dtype=jnp.int32)
    owner = jnp.sum(jnp.where(block_slot == dp_index, numbers, 0))
    flags = jnp.any(owned_rows == owner, axis=1)
    return flags.astype(jnp.float32)


def per_device(queries, kernel_inv, train_grads, candidates, block_slot):
    n_x = lax.axis_size("x")
    n_zc = lax.axis_size("zc")
    n_col = lax.axis_size("col")
    col_index = lax.axis_index("col")
    dp_index = lax.axis_index("x") * n_zc + lax.axis_index("zc")
    per_col = candidates.shape[0] // n_col
    first_row = col_index * per_col
    precond = jnp.dot(queries, kernel_inv, preferred_element_type=jnp.float32).astype(jnp.bfloat16)
    perm = [(a * n_col + b, b * n_col + a) for a in range(n_x) for b in range(n_col)]
    moved = lax.ppermute(precond, ("x", "col"), perm)
    rows = lax.all_gather(moved, "zc", axis=0, tiled=True)
    selected = lax.all_gather(rows, "x", axis=1, tiled=True)
    partial_scores = lax.dot_general(
        selected, train_grads, (((1,), (1,)), ((), ())), preferred_element_type=jnp.float32
    )
    flags = listed_flags(candidates, block_slot, first_row, per_col, dp_index)
    return (partial_scores * flags[:, None]).astype(jnp.bfloat16)


def solution(mesh):
    n_dp, n_col = mesh.devices.shape
    n_x = n_col
    grid = Mesh(mesh.devices.reshape(n_x, n_dp // n_x, n_col), ("x", "zc", "col"))
    rows = ("x", "zc")
    placed = (P(rows, None), P(None, "col"), P(rows, None), P(), P())
    return jax.shard_map(
        per_device, mesh=grid, in_specs=placed, out_specs=P("col", rows), check_vma=False
    )
```

time: 317 us -> 133 us (0.42)
  waiting for transfers between devices: 275 us -> 36.2 us
  blocking collectives: 11 us -> 70.9 us
  local copies, waits for them, and re-layouts: 8.48 us -> 2.35 us
    all_gather x1, waiting for transfers between devices: 275 us -> 36.2 us  [per_device(): selected = lax.all_gather(rows, 'x', axis=1, tiled=True)]
    all_gather x1, blocking collectives: 11 us -> 70.9 us  [per_device(): rows = lax.all_gather(moved, 'zc', axis=0, tiled=True)]
    unnamed x3, local copies, waits for them, and re-layouts: 8.48 us -> 2.35 us
  transfers between devices with their start and end apart: 1 -> 2, of which waited for: 1 -> 1; matrix products, arithmetic and copies ran while one was open for 1% -> 2% of each run, Pallas kernels for 0% -> 0%
where the time goes in v1:
time: 133 us; the launch traced here: 132 us
  blocking collectives  70.9 us (53%)
  waiting for transfers between devices  36.2 us (27%)
  between operations  13.4 us (10%)
  matrix products  5.68 us (4%)
  other arithmetic  3.11 us (2%)
  local copies, waits for them, and re-layouts  2.35 us (2%)
    all_gather x1, blocking collectives, per_device(): rows = lax.all_gather(moved, 'zc', axis=0, tiled=True)  70.9 us
    all_gather x1, waiting for transfers between devices, per_device(): selected = lax.all_gather(rows, 'x', axis=1, tiled=True)  36.2 us
    dot_general x1, matrix products, per_device(): lax.dot_general(selected, train_grads, (((1,), (1,)), ((), ())), preferre...  4.59 us
  transfers between devices with their start and end apart: 2, of which 1 were waited for; matrix products, arithmetic and copies ran while one was open for 2% of the time, Pallas kernels for 0%

profile of v1, /device:TPU:1, one launch (start us, length us, event | category | flops | bytes accessed | tf_op | source)
XLA Modules:
  0.0 132.3 jit_solution(1887286174470788481)
XLA Ops:
  6.5 0.0 copy-start
  6.5 0.0 all-gather.3.cloned.1.call-start
  6.5 1.6 %copy-done = bf16[2048,512]{1,0:T(8,128)(2,1)S(1)} copy-done((bf16[2048,512]{1,0:T(8,128)(2,1)S(1)}, bf16[2048,512]{1,0:T(8,128)(2,1)}, u32[]{:S(2)}) %copy-start) | copy-done | bytes 2097176
  8.1 1.1 convolution_convert_fusion
  9.2 0.7 collective-permute-start
  9.9 0.0 collective-permute-done
  9.9 70.9 %all-gather = bf16[64,4,512]{2,1,0:T(4,128)(2,1)S(1)} all-gather(bf16[1,4,512]{2,1,0:T(4,128)(2,1)S(1)} %bitcast.5), channel_id=1, replica_groups=mesh['x'=4,'zc'=64,'col'=4] {'zc'}, dimensions={0}, use_global_device_ids=true | all-gather | bytes 266240 | tf_op jit(solution)/shard_map/all_gather | solution.py:27
  80.8 0.8 reshape.4
  81.5 0.0 all-gather.3.cloned.1.call-update
  81.5 1.4 %fusion.2 = s32[]{:T(128)} fusion(s32[256]{0:T(256)} %param.9, s32[]{:T(128)S(6)} %add.7), kind=kLoop, calls=%fused_computation.6 | loop fusion | flops 767 | bytes 1032 | tf_op jit(solution)/shard_map/reduce_sum | solution.py:11
  82.9 1.7 %fusion.1 = pred[256]{0:T(512)(128)(4,1)S(1)} fusion(s32[1024,128]{1,0:T(8,128)} %param.8, s32[]{:T(128)S(6)} %select_n.7, s32[]{:T(128)} %fusion.2), kind=kLoop, calls=%fused_computation.4 | loop fusion | flops 65280 | bytes 131336 | tf_op jit(solution)/shard_map/reduce_or | solution.py:12
  84.7 36.2 %all-gather.3.cloned.1.call-done = bf16[256,2048]{1,0:T(8,128)(2,1)} async-done(((bf16[256,512]{1,0:T(8,128)(2,1)}), bf16[256,2048]{1,0:T(8,128)(2,1)}) %all-gather.3.cloned.1.call-update) | async-done | bytes 1048592 | tf_op jit(solution)/shard_map/all_gather | solution.py:28
  120.9 4.6 %fusion = bf16[256,1024]{1,0:T(8,128)(2,1)} fusion(bf16[256,2048]{1,0:T(8,128)(2,1)} %all-gather.3.cloned.1.call-done, bf16[1024,2048]{1,0:T(8,128)(2,1)} %param.7, f32[256]{0:T(256)S(1)} %convert_element_type.14), kind=kOutput, calls=%fused_computation.1 | convolution fusion | flops 1074266112 | bytes 5768192 | tf_op jit(solution)/shard_map/dot_general | solution.py:29
  (1 shorter events, 0.0 us)
Async XLA Ops:
  6.5 1.6 %copy-start = (bf16[2048,512]{1,0:T(8,128)(2,1)S(1)}, bf16[2048,512]{1,0:T(8,128)(2,1)}, u32[]{:S(2)}) copy-start(bf16[2048,512]{1,0:T(8,128)(2,1)} %param.6) | copy-start | bytes 6291460
  6.5 114.3 %all-gather.3.cloned.1.call-start = ((), (), s32[]{:S(2)}) async-start(), calls=%async_computation | async-start | bytes 1310720 | tf_op jit(solution)/shard_map/all_gather | solution.py:28
  9.2 0.7 collective-permute-start
Sparse Core Ops, SparseCore 0:
  81.7 39.1 all-gather.2

commit v2 on v1

--- a/solution.py
+++ b/solution.py
@@ -1,8 +1,108 @@
-import numpy as np
+import functools
+
 import jax
 import jax.numpy as jnp
 from jax import lax
+from jax.experimental import pallas as pl
+from jax.experimental.pallas import tpu as pltpu
 from jax.sharding import Mesh, PartitionSpec as P
+
+MESH = pl.DeviceIdType.MESH
+
+
+def gather_kernel(n_x, n_zc, block_ref, out_ref, held, send_z, recv_z, send_x, recv_x, own_sem):
+    me_x = lax.axis_index("x")
+    me_zc = lax.axis_index("zc")
+    me_y = lax.axis_index("col")
+    width = block_ref.shape[1]
+    cols = pl.ds(pl.multiple_of(me_x * width, width), width)
+
+    barrier = pltpu.get_barrier_semaphore()
+
+    def greet(k, carry):
+        peer = lax.rem(me_zc + k, n_zc)
+        pl.semaphore_signal(barrier, inc=1, device_id=(me_x, peer, me_y), device_id_type=MESH)
+        return carry
+
+    lax.fori_loop(1, n_zc, greet, 0)
+    for k in range(1, n_x):
+        peer = lax.rem(me_x + k, n_x)
+        pl.semaphore_signal(barrier, inc=1, device_id=(peer, me_zc, me_y), device_id_type=MESH)
+    pl.semaphore_wait(barrier, n_zc - 1 + n_x - 1)
+
+    own = pltpu.make_async_copy(block_ref, held.at[me_zc, :, cols], own_sem)
+    own.start()
+
+    def z_copy(src, dst):
+        return pltpu.make_async_remote_copy(
+            src_ref=block_ref,
+            dst_ref=held.at[src, :, cols],
+            send_sem=send_z.at[dst],
+            recv_sem=recv_z.at[src],
+            device_id=(me_x, dst, me_y),
+            device_id_type=MESH,
+        )
+
+    def z_start(k, carry):
+        z_copy(me_zc, lax.rem(me_zc + k, n_zc)).start()
+        return carry
+
+    lax.fori_loop(1, n_zc, z_start, 0)
+    own.wait()
+
+    def z_arrive(k, carry):
+        z_copy(lax.rem(me_zc + k, n_zc), me_zc).wait_recv()
+        return carry
+
+    lax.fori_loop(1, n_zc, z_arrive, 0)
+
+    def x_copy(src, dst):
+        src_cols = pl.ds(pl.multiple_of(src * width, width), width)
+        return pltpu.make_async_remote_copy(
+            src_ref=held.at[:, :, src_cols],
+            dst_ref=held.at[:, :, src_cols],
+            send_sem=send_x.at[dst],
+            recv_sem=recv_x.at[src],
+            device_id=(dst, me_zc, me_y),
+            device_id_type=MESH,
+        )
+
+    for k in range(1, n_x):
+        x_copy(me_x, lax.rem(me_x + k, n_x)).start()
+    for k in range(1, n_x):
+        x_copy(lax.rem(me_x + k, n_x), me_x).wait_recv()
+
+    def z_sent(k, carry):
+        z_copy(me_zc, lax.rem(me_zc + k, n_zc)).wait_send()
+        return carry
+
+    lax.fori_loop(1, n_zc, z_sent, 0)
+    for k in range(1, n_x):
+        x_copy(me_x, lax.rem(me_x + k, n_x)).wait_send()
+    out_ref[...] = held[...]
+
+
+def gather_rows(block, n_x, n_zc):
+    rows, width = block.shape
+    shape = (n_zc, rows, n_x * width)
+    return pl.pallas_call(
+        functools.partial(gather_kernel, n_x, n_zc),
+        out_shape=jax.ShapeDtypeStruct(shape, block.dtype),
+        in_specs=[pl.BlockSpec(memory_space=pltpu.VMEM)],
+        out_specs=pl.BlockSpec(memory_space=pltpu.VMEM),
+        scratch_shapes=[
+            pltpu.VMEM(shape, block.dtype),
+            pltpu.SemaphoreType.DMA((n_zc,)),
+            pltpu.SemaphoreType.DMA((n_zc,)),
+            pltpu.SemaphoreType.DMA((n_x,)),
+            pltpu.SemaphoreType.DMA((n_x,)),
+            pltpu.SemaphoreType.DMA(()),
+        ],
+        compiler_params=pltpu.CompilerParams(collective_id=0, has_side_effects=True),
+        cost_estimate=pl.CostEstimate(
+            flops=0, transcendentals=0, bytes_accessed=2 * n_zc * rows * n_x * width * 2
+        ),
+    )(block)
 
 
 def listed_flags(candidates, block_slot, first_row, row_count, dp_index):
@@ -24,8 +124,8 @@
     precond = jnp.dot(queries, kernel_inv, preferred_element_type=jnp.float32).astype(jnp.bfloat16)
     perm = [(a * n_col + b, b * n_col + a) for a in range(n_x) for b in range(n_col)]
     moved = lax.ppermute(precond, ("x", "col"), perm)
-    rows = lax.all_gather(moved, "zc", axis=0, tiled=True)
-    selected = lax.all_gather(rows, "x", axis=1, tiled=True)
+    gathered = gather_rows(moved, n_x, n_zc)
+    selected = gathered.reshape(per_col, gathered.shape[2])
     partial_scores = lax.dot_general(
         selected, train_grads, (((1,), (1,)), ((), ())), preferred_element_type=jnp.float32
     )

time: 133 us -> 91.5 us (0.69)
  Pallas kernels: 0 us -> 78.6 us
  blocking collectives: 70.9 us -> 0 us
  waiting for transfers between devices: 36.2 us -> 0.01 us
  between operations: 13.4 us -> 0.06 us
    pallas_call x0 -> x1, Pallas kernels: none -> 78.6 us  [gather_rows(): pl.pallas_call(functools.partial(gather_kernel, n_x, n_zc), out_shape=jax...]
    all_gather x1 -> x0, blocking collectives: 70.9 us -> none  [per_device(): rows = lax.all_gather(moved, 'zc', axis=0, tiled=True)]
    all_gather x1 -> x0, waiting for transfers between devices: 36.2 us -> none  [per_device(): selected = lax.all_gather(rows, 'x', axis=1, tiled=True)]
    reshape x0 -> x1, local copies, waits for them, and re-layouts: none -> 1.34 us  [per_device(): selected = gathered.reshape(per_col, gathered.shape[2])]
  transfers between devices with their start and end apart: 2 -> 1, of which waited for: 1 -> 0; matrix products, arithmetic and copies ran while one was open for 2% -> 3% of each run, Pallas kernels for 0% -> 0%
where the time goes in v2:
time: 91.5 us; the launch traced here: 91.1 us
  Pallas kernels  78.6 us (86%)
  matrix products  5.36 us (6%)
  local copies, waits for them, and re-layouts  3.52 us (4%)
  other arithmetic  2.99 us (3%)
    pallas_call x1, Pallas kernels, gather_rows(): pl.pallas_call(functools.partial(gather_kernel, n_x, n_zc), out_shape=jax...  78.6 us
    dot_general x1, matrix products, per_device(): lax.dot_general(selected, train_grads, (((1,), (1,)), ((), ())), preferre...  4.27 us
    unnamed x4, local copies, waits for them, and re-layouts  2.18 us
  transfers between devices with their start and end apart: 1, of which 0 were waited for; matrix products, arithmetic and copies ran while one was open for 3% of the time, Pallas kernels for 0%

profile of v2, /device:TPU:1, one launch (start us, length us, event | category | flops | bytes accessed | tf_op | source)
XLA Modules:
  0.0 91.1 jit_solution(528784663986835685)
XLA Ops:
  0.0 0.0 copy-start
  0.0 1.6 %copy-done = bf16[2048,512]{1,0:T(8,128)(2,1)S(1)} copy-done((bf16[2048,512]{1,0:T(8,128)(2,1)S(1)}, bf16[2048,512]{1,0:T(8,128)(2,1)}, u32[]{:S(2)}) %copy-start) | copy-done | bytes 2097176
  1.6 1.1 %convolution_convert_fusion = bf16[4,512]{1,0:T(4,128)(2,1)S(1)} fusion(bf16[4,2048]{1,0:T(4,128)(2,1)} %param.5, bf16[2048,512]{1,0:T(8,128)(2,1)S(1)} %copy-done), kind=kOutput, calls=%fused_computation.2 | convolution fusion | flops 8390656 | bytes 2117632 | tf_op jit(solution)/shard_map/dot_general | solution.py:124
  2.7 0.7 collective-permute-start
  3.4 1.3 %fusion.2 = s32[]{:T(128)} fusion(s32[256]{0:T(256)} %param.9, s32[]{:T(128)S(6)} %add.7), kind=kLoop, calls=%fused_computation.6 | loop fusion | flops 767 | bytes 1032 | tf_op jit(solution)/shard_map/reduce_sum | solution.py:111
  4.7 1.7 %fusion.1 = pred[256]{0:T(512)(128)(4,1)S(1)} fusion(s32[1024,128]{1,0:T(8,128)} %param.8, s32[]{:T(128)S(6)} %select_n.7, s32[]{:T(128)} %fusion.2), kind=kLoop, calls=%fused_computation.4 | loop fusion | flops 65280 | bytes 131336 | tf_op jit(solution)/shard_map/reduce_or | solution.py:112
  6.4 0.0 collective-permute-done.block_ref
  6.4 0.0 copy-start.1
  6.4 0.6 copy-done.1
  7.0 78.6 %shard_map.55 = bf16[64,4,2048]{2,1,0:T(4,128)(2,1)} custom-call(bf16[4,512]{1,0:T(4,128)(2,1)} %copy-done.1), custom_call_target="tpu_custom_call" | custom-call | bytes 2097152 | tf_op jit(solution)/shard_map/pallas_call | solution.py:88
  85.5 1.3 %reshape.6 = bf16[256,2048]{1,0:T(8,128)(2,1)S(1)} reshape(bf16[64,4,2048]{2,1,0:T(4,128)(2,1)} %shard_map.55) | data formatting | bytes 2097152 | tf_op jit(solution)/shard_map/reshape | solution.py:128
  86.9 4.3 %fusion = bf16[256,1024]{1,0:T(8,128)(2,1)} fusion(bf16[256,2048]{1,0:T(8,128)(2,1)S(1)} %reshape.6, bf16[1024,2048]{1,0:T(8,128)(2,1)} %param.7, f32[256]{0:T(256)S(1)} %convert_element_type.14), kind=kOutput, calls=%fused_computation.1 | convolution fusion | flops 1074266112 | bytes 5768192 | tf_op jit(solution)/shard_map/dot_general | solution.py:129
  (1 shorter events, 0.0 us)
Async XLA Ops:
  0.0 1.6 %copy-start = (bf16[2048,512]{1,0:T(8,128)(2,1)S(1)}, bf16[2048,512]{1,0:T(8,128)(2,1)}, u32[]{:S(2)}) copy-start(bf16[2048,512]{1,0:T(8,128)(2,1)} %param.6) | copy-start | bytes 6291460
  2.7 3.7 %collective-permute-start = (bf16[4,512]{1,0:T(4,128)(2,1)S(1)}, bf16[4,512]{1,0:T(4,128)(2,1)S(1)}, u32[]{:S(2)}, u32[]{:S(2)}) collective-permute-start(bf16[4,512]{1,0:T(4,128)(2,1)S(1)} %convolution_convert_fusion), channel_id=1, source_target_pairs={{0,0},{1,256},{2,512},{3,768},{256,1},{257,257},{258,513},{259,769... | collective-permute-start | bytes 12296 | tf_op jit(solution)/shard_map/ppermute | solution.py:126
  6.4 0.6 copy-start.1

commit v3 on v1

--- a/solution.py
+++ b/solution.py
@@ -1,8 +1,127 @@
-import numpy as np
+import functools
+
 import jax
 import jax.numpy as jnp
 from jax import lax
+from jax.experimental import pallas as pl
+from jax.experimental.pallas import tpu as pltpu
 from jax.sharding import Mesh, PartitionSpec as P
+
+MESH = pl.DeviceIdType.MESH
+
+
+def gather_kernel(n_x, n_z, block_ref, out_ref, held, send_ring, recv_ring, send_pair, recv_pair,
+                  send_x, recv_x, own_sem):
+    me_x = lax.axis_index("x")
+    me_zc = lax.axis_index("zc")
+    me_y = lax.axis_index("col")
+    me_z = me_zc // 2
+    lane = me_zc % 2
+    width = block_ref.shape[1]
+    cols = pl.ds(pl.multiple_of(me_x * width, width), width)
+    reach = (n_z // 2, (n_z - 1) // 2)
+    nexts = (lax.rem(me_z + 1, n_z) * 2 + lane, lax.rem(me_z + n_z - 1, n_z) * 2 + lane)
+    pair = me_z * 2 + 1 - lane
+    x_peers = [(k, lax.rem(me_x + k, n_x)) for k in range(1, n_x)]
+
+    barrier = pltpu.get_barrier_semaphore()
+    peers = [(me_x, nexts[0], me_y), (me_x, nexts[1], me_y), (me_x, pair, me_y)]
+    peers += [(px, me_z * 2 + other, me_y) for _, px in x_peers for other in range(2)]
+    for peer in peers:
+        pl.semaphore_signal(barrier, inc=1, device_id=peer, device_id_type=MESH)
+    pl.semaphore_wait(barrier, len(peers))
+
+    own = pltpu.make_async_copy(block_ref, held.at[me_zc, :, cols], own_sem)
+    own.start()
+
+    def slot_of(way, hops):
+        origin = me_z - hops if way == 0 else me_z + hops
+        return lax.rem(origin + n_z, n_z) * 2 + lane
+
+    def ring_copy(way, step, source, slot):
+        return pltpu.make_async_remote_copy(
+            src_ref=source, dst_ref=held.at[slot, :, cols],
+            send_sem=send_ring.at[way, step], recv_sem=recv_ring.at[way, step],
+            device_id=(me_x, nexts[way], me_y), device_id_type=MESH)
+
+    def spread(source, slot):
+        dst = held.at[slot, :, cols]
+        pltpu.make_async_remote_copy(
+            src_ref=source, dst_ref=dst, send_sem=send_pair, recv_sem=recv_pair,
+            device_id=(me_x, pair, me_y), device_id_type=MESH).start()
+        for k, px in x_peers:
+            for other in range(2):
+                pltpu.make_async_remote_copy(
+                    src_ref=source, dst_ref=dst, send_sem=send_x.at[k, other],
+                    recv_sem=recv_x.at[n_x - k, lane],
+                    device_id=(px, me_z * 2 + other, me_y), device_id_type=MESH).start()
+
+    for way in range(2):
+        if reach[way] >= 1:
+            ring_copy(way, 1, block_ref, me_zc).start()
+    spread(block_ref, me_zc)
+
+    def step_body(step, ways, forward):
+        for way in ways:
+            slot = slot_of(way, step)
+            ring_copy(way, step, held.at[slot, :, cols], slot).wait_recv()
+            if forward[way]:
+                ring_copy(way, step + 1, held.at[slot, :, cols], slot).start()
+        for way in ways:
+            slot = slot_of(way, step)
+            spread(held.at[slot, :, cols], slot)
+
+    def both(step, carry):
+        step_body(step, (0, 1), (True, True))
+        return carry
+
+    lax.fori_loop(1, reach[1], both, 0)
+    if reach[1] >= 1:
+        step_body(reach[1], (0, 1), (reach[1] < reach[0], False))
+    if reach[0] > reach[1]:
+        step_body(reach[0], (0,), (False, False))
+
+    for way in range(2):
+        for step in range(1, reach[way] + 1):
+            slot = slot_of(way, step - 1)
+            ring_copy(way, step, held.at[slot, :, cols], slot).wait_send()
+    line = held.at[pl.ds(0, n_z), :, cols]
+    pltpu.make_async_remote_copy(
+        src_ref=line, dst_ref=line, send_sem=send_pair, recv_sem=recv_pair,
+        device_id=(me_x, pair, me_y), device_id_type=MESH).wait()
+    for k, px in x_peers:
+        for other in range(2):
+            pltpu.make_async_remote_copy(
+                src_ref=line, dst_ref=line, send_sem=send_x.at[k, other], recv_sem=recv_x.at[k, other],
+                device_id=(px, me_z * 2 + other, me_y), device_id_type=MESH).wait()
+    own.wait()
+    out_ref[...] = held[...]
+
+
+def gather_rows(block, n_x, n_zc):
+    rows, width = block.shape
+    n_z = n_zc // 2
+    shape = (n_zc, rows, n_x * width)
+    return pl.pallas_call(
+        functools.partial(gather_kernel, n_x, n_z),
+        out_shape=jax.ShapeDtypeStruct(shape, block.dtype),
+        in_specs=[pl.BlockSpec(memory_space=pltpu.VMEM)],
+        out_specs=pl.BlockSpec(memory_space=pltpu.VMEM),
+        scratch_shapes=[
+            pltpu.VMEM(shape, block.dtype),
+            pltpu.SemaphoreType.DMA((2, n_z // 2 + 1)),
+            pltpu.SemaphoreType.DMA((2, n_z // 2 + 1)),
+            pltpu.SemaphoreType.DMA(()),
+            pltpu.SemaphoreType.DMA(()),
+            pltpu.SemaphoreType.DMA((n_x, 2)),
+            pltpu.SemaphoreType.DMA((n_x, 2)),
+            pltpu.SemaphoreType.DMA(()),
+        ],
+        compiler_params=pltpu.CompilerParams(collective_id=0, has_side_effects=True),
+        cost_estimate=pl.CostEstimate(
+            flops=0, transcendentals=0, bytes_accessed=2 * n_zc * rows * n_x * width * 2
+        ),
+    )(block)
 
 
 def listed_flags(candidates, block_slot, first_row, row_count, dp_index):
@@ -24,8 +143,8 @@
     precond = jnp.dot(queries, kernel_inv, preferred_element_type=jnp.float32).astype(jnp.bfloat16)
     perm = [(a * n_col + b, b * n_col + a) for a in range(n_x) for b in range(n_col)]
     moved = lax.ppermute(precond, ("x", "col"), perm)
-    rows = lax.all_gather(moved, "zc", axis=0, tiled=True)
-    selected = lax.all_gather(rows, "x", axis=1, tiled=True)
+    gathered = gather_rows(moved, n_x, n_zc)
+    selected = gathered.reshape(per_col, gathered.shape[2])
     partial_scores = lax.dot_general(
         selected, train_grads, (((1,), (1,)), ((), ())), preferred_element_type=jnp.float32
     )

time: 133 us -> 89.6 us (0.67)
  Pallas kernels: 0 us -> 76.6 us
  blocking collectives: 70.9 us -> 0 us
  waiting for transfers between devices: 36.2 us -> 0.01 us
  between operations: 13.4 us -> 0.06 us
    pallas_call x0 -> x1, Pallas kernels: none -> 76.6 us  [gather_rows(): pl.pallas_call(functools.partial(gather_kernel, n_x, n_z), out_shape=jax....]
    all_gather x1 -> x0, blocking collectives: 70.9 us -> none  [per_device(): rows = lax.all_gather(moved, 'zc', axis=0, tiled=True)]
    all_gather x1 -> x0, waiting for transfers between devices: 36.2 us -> none  [per_device(): selected = lax.all_gather(rows, 'x', axis=1, tiled=True)]
    reshape x0 -> x1, local copies, waits for them, and re-layouts: none -> 1.34 us  [per_device(): selected = gathered.reshape(per_col, gathered.shape[2])]
  transfers between devices with their start and end apart: 2 -> 1, of which waited for: 1 -> 0; matrix products, arithmetic and copies ran while one was open for 2% -> 3% of each run, Pallas kernels for 0% -> 0%
where the time goes in v3:
time: 89.6 us; the launch traced here: 89.2 us
  Pallas kernels  76.6 us (85%)
  matrix products  5.36 us (6%)
  local copies, waits for them, and re-layouts  3.52 us (4%)
  other arithmetic  2.99 us (3%)
    pallas_call x1, Pallas kernels, gather_rows(): pl.pallas_call(functools.partial(gather_kernel, n_x, n_z), out_shape=jax....  76.6 us
    dot_general x1, matrix products, per_device(): lax.dot_general(selected, train_grads, (((1,), (1,)), ((), ())), preferre...  4.27 us
    unnamed x4, local copies, waits for them, and re-layouts  2.18 us
  transfers between devices with their start and end apart: 1, of which 0 were waited for; matrix products, arithmetic and copies ran while one was open for 3% of the time, Pallas kernels for 0%

profile of v3, /device:TPU:1, one launch (start us, length us, event | category | flops | bytes accessed | tf_op | source)
XLA Modules:
  0.0 89.2 jit_solution(15963154001738526351)
XLA Ops:
  0.0 0.0 copy-start
  0.0 1.6 %copy-done = bf16[2048,512]{1,0:T(8,128)(2,1)S(1)} copy-done((bf16[2048,512]{1,0:T(8,128)(2,1)S(1)}, bf16[2048,512]{1,0:T(8,128)(2,1)}, u32[]{:S(2)}) %copy-start) | copy-done | bytes 2097176
  1.6 1.1 %convolution_convert_fusion = bf16[4,512]{1,0:T(4,128)(2,1)S(1)} fusion(bf16[4,2048]{1,0:T(4,128)(2,1)} %param.5, bf16[2048,512]{1,0:T(8,128)(2,1)S(1)} %copy-done), kind=kOutput, calls=%fused_computation.2 | convolution fusion | flops 8390656 | bytes 2117632 | tf_op jit(solution)/shard_map/dot_general | solution.py:143
  2.7 0.7 collective-permute-start
  3.4 1.3 %fusion.2 = s32[]{:T(128)} fusion(s32[256]{0:T(256)} %param.9, s32[]{:T(128)S(6)} %add.7), kind=kLoop, calls=%fused_computation.6 | loop fusion | flops 767 | bytes 1032 | tf_op jit(solution)/shard_map/reduce_sum | solution.py:130
  4.7 1.7 %fusion.1 = pred[256]{0:T(512)(128)(4,1)S(1)} fusion(s32[1024,128]{1,0:T(8,128)} %param.8, s32[]{:T(128)S(6)} %select_n.7, s32[]{:T(128)} %fusion.2), kind=kLoop, calls=%fused_computation.4 | loop fusion | flops 65280 | bytes 131336 | tf_op jit(solution)/shard_map/reduce_or | solution.py:131
  6.4 0.0 collective-permute-done.block_ref
  6.4 0.0 copy-start.1
  6.4 0.6 copy-done.1
  7.0 76.6 %shard_map.55 = bf16[64,4,2048]{2,1,0:T(4,128)(2,1)} custom-call(bf16[4,512]{1,0:T(4,128)(2,1)} %copy-done.1), custom_call_target="tpu_custom_call" | custom-call | bytes 2097152 | tf_op jit(solution)/shard_map/pallas_call | solution.py:105
  83.6 1.3 %reshape.6 = bf16[256,2048]{1,0:T(8,128)(2,1)S(1)} reshape(bf16[64,4,2048]{2,1,0:T(4,128)(2,1)} %shard_map.55) | data formatting | bytes 2097152 | tf_op jit(solution)/shard_map/reshape | solution.py:147
  84.9 4.3 %fusion = bf16[256,1024]{1,0:T(8,128)(2,1)} fusion(bf16[256,2048]{1,0:T(8,128)(2,1)S(1)} %reshape.6, bf16[1024,2048]{1,0:T(8,128)(2,1)} %param.7, f32[256]{0:T(256)S(1)} %convert_element_type.14), kind=kOutput, calls=%fused_computation.1 | convolution fusion | flops 1074266112 | bytes 5768192 | tf_op jit(solution)/shard_map/dot_general | solution.py:148
  (1 shorter events, 0.0 us)
Async XLA Ops:
  0.0 1.6 %copy-start = (bf16[2048,512]{1,0:T(8,128)(2,1)S(1)}, bf16[2048,512]{1,0:T(8,128)(2,1)}, u32[]{:S(2)}) copy-start(bf16[2048,512]{1,0:T(8,128)(2,1)} %param.6) | copy-start | bytes 6291460
  2.7 3.7 %collective-permute-start = (bf16[4,512]{1,0:T(4,128)(2,1)S(1)}, bf16[4,512]{1,0:T(4,128)(2,1)S(1)}, u32[]{:S(2)}, u32[]{:S(2)}) collective-permute-start(bf16[4,512]{1,0:T(4,128)(2,1)S(1)} %convolution_convert_fusion), channel_id=1, source_target_pairs={{0,0},{1,256},{2,512},{3,768},{256,1},{257,257},{258,513},{259,769... | collective-permute-start | bytes 12296 | tf_op jit(solution)/shard_map/ppermute | solution.py:145
  6.4 0.6 copy-start.1

commit v4 on v1

--- a/solution.py
+++ b/solution.py
@@ -1,8 +1,114 @@
-import numpy as np
+import functools
+
 import jax
 import jax.numpy as jnp
 from jax import lax
+from jax.experimental import pallas as pl
+from jax.experimental.pallas import tpu as pltpu
 from jax.sharding import Mesh, PartitionSpec as P
+
+MESH = pl.DeviceIdType.MESH
+
+
+def gather_kernel(n_x, n_z, block_ref, out_ref, held, send_z, recv_z, send_x, recv_x, send_pair,
+                  recv_pair, own_sem):
+    me_x = lax.axis_index("x")
+    me_zc = lax.axis_index("zc")
+    me_y = lax.axis_index("col")
+    me_z = me_zc // 2
+    lane = me_zc % 2
+    pair = me_z * 2 + 1 - lane
+    z_peers = [(k, lax.rem(me_z + k, n_z) * 2 + lane) for k in range(1, n_z)]
+    x_peers = [(k, lax.rem(me_x + k, n_x)) for k in range(1, n_x)]
+
+    barrier = pltpu.get_barrier_semaphore()
+    peers = [(me_x, zc, me_y) for _, zc in z_peers] + [(px, me_zc, me_y) for _, px in x_peers]
+    peers.append((me_x, pair, me_y))
+    for peer in peers:
+        pl.semaphore_signal(barrier, inc=1, device_id=peer, device_id_type=MESH)
+    pl.semaphore_wait(barrier, len(peers))
+
+    own = pltpu.make_async_copy(block_ref, held.at[me_x, lane, me_z], own_sem)
+    own.start()
+
+    def z_copy(k, zc):
+        return pltpu.make_async_remote_copy(
+            src_ref=block_ref, dst_ref=held.at[me_x, lane, me_z],
+            send_sem=send_z.at[k], recv_sem=recv_z.at[n_z - k],
+            device_id=(me_x, zc, me_y), device_id_type=MESH)
+
+    for k, zc in z_peers:
+        z_copy(k, zc).start()
+    for k, zc in z_peers:
+        src_z = lax.rem(me_z + k, n_z)
+        pltpu.make_async_remote_copy(
+            src_ref=block_ref, dst_ref=held.at[me_x, lane, src_z],
+            send_sem=send_z.at[k], recv_sem=recv_z.at[k],
+            device_id=(me_x, zc, me_y), device_id_type=MESH).wait_recv()
+    own.wait()
+
+    def to_pair(c, index):
+        line = held.at[c, lane]
+        return pltpu.make_async_remote_copy(
+            src_ref=line, dst_ref=line, send_sem=send_pair.at[index], recv_sem=recv_pair.at[index],
+            device_id=(me_x, pair, me_y), device_id_type=MESH)
+
+    def x_copy(k, px):
+        line = held.at[me_x, lane]
+        return pltpu.make_async_remote_copy(
+            src_ref=line, dst_ref=line, send_sem=send_x.at[k], recv_sem=recv_x.at[n_x - k],
+            device_id=(px, me_zc, me_y), device_id_type=MESH)
+
+    to_pair(me_x, 0).start()
+    for k, px in x_peers:
+        x_copy(k, px).start()
+    for k, px in x_peers:
+        line = held.at[px, lane]
+        pltpu.make_async_remote_copy(
+            src_ref=line, dst_ref=line, send_sem=send_x.at[k], recv_sem=recv_x.at[k],
+            device_id=(px, me_zc, me_y), device_id_type=MESH).wait_recv()
+        to_pair(px, k).start()
+
+    for index in range(n_x):
+        c = me_x if index == 0 else x_peers[index - 1][1]
+        line = held.at[c, 1 - lane]
+        pltpu.make_async_remote_copy(
+            src_ref=line, dst_ref=line, send_sem=send_pair.at[index], recv_sem=recv_pair.at[index],
+            device_id=(me_x, pair, me_y), device_id_type=MESH).wait_recv()
+
+    for k, zc in z_peers:
+        z_copy(k, zc).wait_send()
+    for k, px in x_peers:
+        x_copy(k, px).wait_send()
+    to_pair(me_x, 0).wait_send()
+    for k, px in x_peers:
+        to_pair(px, k).wait_send()
+    out_ref[...] = held[...]
+
+
+def gather_rows(block, n_x, n_zc):
+    n_z = n_zc // 2
+    shape = (n_x, 2, n_z) + block.shape
+    return pl.pallas_call(
+        functools.partial(gather_kernel, n_x, n_z),
+        out_shape=jax.ShapeDtypeStruct(shape, block.dtype),
+        in_specs=[pl.BlockSpec(memory_space=pltpu.VMEM)],
+        out_specs=pl.BlockSpec(memory_space=pltpu.VMEM),
+        scratch_shapes=[
+            pltpu.VMEM(shape, block.dtype),
+            pltpu.SemaphoreType.DMA((n_z,)),
+            pltpu.SemaphoreType.DMA((n_z,)),
+            pltpu.SemaphoreType.DMA((n_x,)),
+            pltpu.SemaphoreType.DMA((n_x,)),
+            pltpu.SemaphoreType.DMA((n_x,)),
+            pltpu.SemaphoreType.DMA((n_x,)),
+            pltpu.SemaphoreType.DMA(()),
+        ],
+        compiler_params=pltpu.CompilerParams(collective_id=0, has_side_effects=True),
+        cost_estimate=pl.CostEstimate(
+            flops=0, transcendentals=0, bytes_accessed=2 * n_x * n_zc * block.size * 2
+        ),
+    )(block)
 
 
 def listed_flags(candidates, block_slot, first_row, row_count, dp_index):
@@ -23,9 +129,12 @@
     first_row = col_index * per_col
     precond = jnp.dot(queries, kernel_inv, preferred_element_type=jnp.float32).astype(jnp.bfloat16)
     perm = [(a * n_col + b, b * n_col + a) for a in range(n_x) for b in range(n_col)]
-    moved = lax.ppermute(precond, ("x", "col"), perm)
-    rows = lax.all_gather(moved, "zc", axis=0, tiled=True)
-    selected = lax.all_gather(rows, "x", axis=1, tiled=True)
+    rows, width = precond.shape
+    tile = precond.reshape(rows * width // 128, 128)
+    moved = lax.ppermute(tile, ("x", "col"), perm)
+    held = gather_rows(moved, n_x, n_zc)
+    held = held.reshape(n_x, 2, n_zc // 2, rows, width // 128, 128)
+    selected = jnp.transpose(held, (2, 1, 3, 0, 4, 5)).reshape(per_col, n_x * width)
     partial_scores = lax.dot_general(
         selected, train_grads, (((1,), (1,)), ((), ())), preferred_element_type=jnp.float32
     )

time: 133 us -> 76.6 us (0.58)
  blocking collectives: 70.9 us -> 0 us
  Pallas kernels: 0 us -> 61.2 us
  waiting for transfers between devices: 36.2 us -> 0.01 us
  between operations: 13.4 us -> 0.06 us
  local copies, waits for them, and re-layouts: 2.35 us -> 5.61 us
    all_gather x1 -> x0, blocking collectives: 70.9 us -> none  [per_device(): rows = lax.all_gather(moved, 'zc', axis=0, tiled=True)]
    pallas_call x0 -> x1, Pallas kernels: none -> 61.2 us  [gather_rows(): pl.pallas_call(functools.partial(gather_kernel, n_x, n_z), out_shape=jax....]
    all_gather x1 -> x0, waiting for transfers between devices: 36.2 us -> none  [per_device(): selected = lax.all_gather(rows, 'x', axis=1, tiled=True)]
    reshape x0 -> x3, local copies, waits for them, and re-layouts: none -> 3.43 us  [the longest x1 1.79 us: per_device(): held = held.reshape(n_x, 2, n_zc // 2, rows, width // 128, 128)]
  transfers between devices with their start and end apart: 2 -> 1, of which waited for: 1 -> 0; matrix products, arithmetic and copies ran while one was open for 2% -> 4% of each run, Pallas kernels for 0% -> 0%
where the time goes in v4:
time: 76.6 us; the launch traced here: 76.2 us
  Pallas kernels  61.2 us (80%)
  matrix products  5.68 us (7%)
  local copies, waits for them, and re-layouts  5.61 us (7%)
  other arithmetic  2.99 us (4%)
    pallas_call x1, Pallas kernels, gather_rows(): pl.pallas_call(functools.partial(gather_kernel, n_x, n_z), out_shape=jax....  61.2 us
    dot_general x1, matrix products, per_device(): lax.dot_general(selected, train_grads, (((1,), (1,)), ((), ())), preferre...  4.59 us
    unnamed x4, local copies, waits for them, and re-layouts  2.18 us
    reshape x1, local copies, waits for them, and re-layouts, per_device(): held = held.reshape(n_x, 2, n_zc // 2, rows, width // 128, 128)  1.79 us
    reduce_or x1, other arithmetic, listed_flags(): flags = jnp.any(owned_rows == owner, axis=1)  1.66 us
    reshape x1, local copies, waits for them, and re-layouts, per_device(): jnp.transpose(held, (2, 1, 3, 0, 4, 5)).reshape(per_col, n_x * width)  1.62 us
  transfers between devices with their start and end apart: 1, of which 0 were waited for; matrix products, arithmetic and copies ran while one was open for 4% of the time, Pallas kernels for 0%

profile of v4, /device:TPU:1, one launch (start us, length us, event | category | flops | bytes accessed | tf_op | source)
XLA Modules:
  0.0 76.2 jit_solution(5211443567309493997)
XLA Ops:
  0.0 0.0 copy-start
  0.0 1.6 %copy-done = bf16[2048,512]{1,0:T(8,128)(2,1)S(1)} copy-done((bf16[2048,512]{1,0:T(8,128)(2,1)S(1)}, bf16[2048,512]{1,0:T(8,128)(2,1)}, u32[]{:S(2)}) %copy-start) | copy-done | bytes 2097176
  1.6 1.1 %convolution_convert_fusion = bf16[4,512]{1,0:T(4,128)(2,1)S(1)} fusion(bf16[4,2048]{1,0:T(4,128)(2,1)} %param.5, bf16[2048,512]{1,0:T(8,128)(2,1)S(1)} %copy-done), kind=kOutput, calls=%fused_computation.2 | convolution fusion | flops 8390656 | bytes 2117632 | tf_op jit(solution)/shard_map/dot_general | solution.py:130
  2.7 0.7 collective-permute-start
  3.4 1.3 %fusion.2 = s32[]{:T(128)} fusion(s32[256]{0:T(256)} %param.9, s32[]{:T(128)S(6)} %add.7), kind=kLoop, calls=%fused_computation.7 | loop fusion | flops 767 | bytes 1032 | tf_op jit(solution)/shard_map/reduce_sum | solution.py:117
  4.7 1.7 %fusion.1 = pred[256]{0:T(512)(128)(4,1)S(1)} fusion(s32[1024,128]{1,0:T(8,128)} %param.8, s32[]{:T(128)S(6)} %select_n.7, s32[]{:T(128)} %fusion.2), kind=kLoop, calls=%fused_computation.5 | loop fusion | flops 65280 | bytes 131336 | tf_op jit(solution)/shard_map/reduce_or | solution.py:118
  6.4 0.0 collective-permute-done.block_ref
  6.4 0.0 copy-start.1
  6.4 0.6 copy-done.1
  7.0 61.2 %shard_map.55 = bf16[4,2,32,16,128]{4,3,2,1,0:T(8,128)(2,1)} custom-call(bf16[16,128]{1,0:T(8,128)(2,1)} %copy-done.1), custom_call_target="tpu_custom_call" | custom-call | bytes 2097152 | tf_op jit(solution)/shard_map/pallas_call | solution.py:92
  68.2 1.8 %copy.8 = bf16[4,2,32,4,4,128]{5,4,0,3,1,2:T(4,128)(2,1)S(1)} copy(bf16[4,2,32,4,4,128]{5,4,3,2,1,0:T(4,128)(2,1)} %bitcast.8) | data formatting | bytes 2097152 | tf_op jit(solution)/shard_map/reshape | solution.py:136
  70.0 1.6 %reshape.14 = bf16[256,2048]{1,0:T(8,128)(2,1)} reshape(bf16[32,2,4,4,4,128]{5,4,3,2,1,0:T(4,128)(2,1)S(1)} %bitcast.9) | data formatting | bytes 2097152 | tf_op jit(solution)/shard_map/reshape | solution.py:137
  71.6 4.6 %fusion = bf16[256,1024]{1,0:T(8,128)(2,1)} fusion(bf16[256,2048]{1,0:T(8,128)(2,1)} %reshape.14, bf16[1024,2048]{1,0:T(8,128)(2,1)} %param.7, f32[256]{0:T(256)S(1)} %convert_element_type.14), kind=kOutput, calls=%fused_computation.1 | convolution fusion | flops 1074266112 | bytes 5768192 | tf_op jit(solution)/shard_map/dot_general | solution.py:138
  (2 shorter events, 0.0 us)
Async XLA Ops:
  0.0 1.6 %copy-start = (bf16[2048,512]{1,0:T(8,128)(2,1)S(1)}, bf16[2048,512]{1,0:T(8,128)(2,1)}, u32[]{:S(2)}) copy-start(bf16[2048,512]{1,0:T(8,128)(2,1)} %param.6) | copy-start | bytes 6291460
  2.7 3.7 %collective-permute-start = (bf16[16,128]{1,0:T(8,128)(2,1)S(1)}, bf16[16,128]{1,0:T(8,128)(2,1)S(1)}, u32[]{:S(2)}, u32[]{:S(2)}) collective-permute-start(bf16[16,128]{1,0:T(8,128)(2,1)S(1)} %reshape.12), channel_id=1, source_target_pairs={{0,0},{1,256},{2,512},{3,768},{256,1},{257,257},{258,513},{259,769... | collective-permute-start | bytes 12296 | tf_op jit(solution)/shard_map/ppermute | solution.py:134
  6.4 0.6 copy-start.1

commit v5 on v4

v5 whole, which is shorter than its diff:
```python
import functools

import jax
import jax.numpy as jnp
from jax import lax
from jax.experimental import pallas as pl
from jax.experimental.pallas import tpu as pltpu
from jax.sharding import Mesh, PartitionSpec as P

MESH = pl.DeviceIdType.MESH


def gather_kernel(n_x, n_z, block_ref, cand_ref, slot_ref, out_ref, flags_ref, held, send_z, recv_z,
                  send_x, recv_x, send_pair, recv_pair, own_sem):
    me_x = lax.axis_index("x")
    me_zc = lax.axis_index("zc")
    me_y = lax.axis_index("col")
    me_z = me_zc // 2
    lane = me_zc % 2
    pair = me_z * 2 + 1 - lane
    on_diagonal = me_x == me_y
    z_peers = [(k, lax.rem(me_z + k, n_z) * 2 + lane) for k in range(1, n_z)]
    x_peers = [(k, lax.rem(me_x + k, n_x)) for k in range(1, n_x)]

    barrier = pltpu.get_barrier_semaphore()
    peers = [(me_y, zc, me_x) for _, zc in z_peers] + [(px, me_zc, me_y) for _, px in x_peers]
    peers.append((me_x, pair, me_y))
    for peer in peers:
        pl.semaphore_signal(barrier, inc=1, device_id=peer, device_id_type=MESH)

    @pl.when(jnp.logical_not(on_diagonal))
    def _():
        pl.semaphore_signal(barrier, inc=1, device_id=(me_y, me_zc, me_x), device_id_type=MESH)

    pl.semaphore_wait(barrier, len(peers) + jnp.where(on_diagonal, 0, 1))

    def z_copy(k, zc):
        return pltpu.make_async_remote_copy(
            src_ref=block_ref, dst_ref=held.at[me_y, lane, me_z],
            send_sem=send_z.at[k], recv_sem=recv_z.at[lax.rem(n_z - k, n_z)],
            device_id=(me_y, zc, me_x), device_id_type=MESH)

    for k, zc in z_peers:
        z_copy(k, zc).start()
    own = pltpu.make_async_copy(block_ref, held.at[me_x, lane, me_z], own_sem)

    @pl.when(on_diagonal)
    def _():
        own.start()

    @pl.when(jnp.logical_not(on_diagonal))
    def _():
        z_copy(0, me_zc).start()

    rows = flags_ref.shape[0]
    slots = slot_ref[...]
    number = lax.broadcasted_iota(jnp.int32, slots.shape, 0) * slots.shape[1]
    number = number + lax.broadcasted_iota(jnp.int32, slots.shape, 1)
    owner = jnp.sum(jnp.where(slots == me_x * (2 * n_z) + me_zc, number, 0), keepdims=True)
    listed = cand_ref[pl.ds(pl.multiple_of(me_y * rows, rows), rows), :] == owner
    flags_ref[...] = jnp.max(listed.astype(jnp.float32), axis=1, keepdims=True)

    for k in range(n_z):
        src_z = lax.rem(me_z + k, n_z)
        src_zc = src_z * 2 + lane
        if k == 0:
            @pl.when(on_diagonal)
            def _():
                own.wait()

            @pl.when(jnp.logical_not(on_diagonal))
            def _():
                pltpu.make_async_remote_copy(
                    src_ref=block_ref, dst_ref=held.at[me_x, lane, src_z],
                    send_sem=send_z.at[0], recv_sem=recv_z.at[0],
                    device_id=(me_y, src_zc, me_x), device_id_type=MESH).wait_recv()
        else:
            pltpu.make_async_remote_copy(
                src_ref=block_ref, dst_ref=held.at[me_x, lane, src_z],
                send_sem=send_z.at[k], recv_sem=recv_z.at[k],
                device_id=(me_y, src_zc, me_x), device_id_type=MESH).wait_recv()

    def to_pair(c, index):
        line = held.at[c, lane]
        return pltpu.make_async_remote_copy(
            src_ref=line, dst_ref=line, send_sem=send_pair.at[index], recv_sem=recv_pair.at[index],
            device_id=(me_x, pair, me_y), device_id_type=MESH)

    def x_copy(k, px):
        line = held.at[me_x, lane]
        return pltpu.make_async_remote_copy(
            src_ref=line, dst_ref=line, send_sem=send_x.at[k], recv_sem=recv_x.at[n_x - k],
            device_id=(px, me_zc, me_y), device_id_type=MESH)

    to_pair(me_x, 0).start()
    for k, px in x_peers:
        x_copy(k, px).start()
    for k, px in x_peers:
        line = held.at[px, lane]
        pltpu.make_async_remote_copy(
            src_ref=line, dst_ref=line, send_sem=send_x.at[k], recv_sem=recv_x.at[k],
            device_id=(px, me_zc, me_y), device_id_type=MESH).wait_recv()
        to_pair(px, k).start()

    for index in range(n_x):
        c = me_x if index == 0 else x_peers[index - 1][1]
        line = held.at[c, 1 - lane]
        pltpu.make_async_remote_copy(
            src_ref=line, dst_ref=line, send_sem=send_pair.at[index], recv_sem=recv_pair.at[index],
            device_id=(me_x, pair, me_y), device_id_type=MESH).wait_recv()

    for k, zc in z_peers:
        z_copy(k, zc).wait_send()

    @pl.when(jnp.logical_not(on_diagonal))
    def _():
        z_copy(0, me_zc).wait_send()

    for k, px in x_peers:
        x_copy(k, px).wait_send()
    to_pair(me_x, 0).wait_send()
    for k, px in x_peers:
        to_pair(px, k).wait_send()
    out_ref[...] = held[...]


def gather_rows(block, candidates, block_slot, n_x, n_zc, rows):
    n_z = n_zc // 2
    shape = (n_x, 2, n_z) + block.shape
    slots = block_slot.reshape(-1, 128) if block_slot.size % 128 == 0 else block_slot.reshape(1, -1)
    return pl.pallas_call(
        functools.partial(gather_kernel, n_x, n_z),
        out_shape=(
            jax.ShapeDtypeStruct(shape, block.dtype),
            jax.ShapeDtypeStruct((rows, 1), jnp.float32),
        ),
        in_specs=[pl.BlockSpec(memory_space=pltpu.VMEM)] * 3,
        out_specs=(pl.BlockSpec(memory_space=pltpu.VMEM), pl.BlockSpec(memory_space=pltpu.VMEM)),
        scratch_shapes=[
            pltpu.VMEM(shape, block.dtype),
            pltpu.SemaphoreType.DMA((n_z,)),
            pltpu.SemaphoreType.DMA((n_z,)),
            pltpu.SemaphoreType.DMA((n_x,)),
            pltpu.SemaphoreType.DMA((n_x,)),
            pltpu.SemaphoreType.DMA((n_x,)),
            pltpu.SemaphoreType.DMA((n_x,)),
            pltpu.SemaphoreType.DMA(()),
        ],
        compiler_params=pltpu.CompilerParams(collective_id=0, has_side_effects=True),
        cost_estimate=pl.CostEstimate(
            flops=0, transcendentals=0, bytes_accessed=2 * n_x * n_zc * block.size * 2
        ),
    )(block, candidates, slots)


def per_device(queries, kernel_inv, train_grads, candidates, block_slot):
    n_x = lax.axis_size("x")
    n_zc = lax.axis_size("zc")
    n_col = lax.axis_size("col")
    per_col = candidates.shape[0] // n_col
    precond = jnp.dot(queries, kernel_inv, preferred_element_type=jnp.float32).astype(jnp.bfloat16)
    rows, width = precond.shape
    tile = precond.reshape(rows * width // 128, 128)
    held, flags = gather_rows(tile, candidates, block_slot, n_x, n_zc, per_col)
    held = held.reshape(n_x, 2, n_zc // 2, rows, width // 128, 128)
    selected = jnp.transpose(held, (2, 1, 3, 0, 4, 5)).reshape(per_col, n_x * width)
    partial_scores = lax.dot_general(
        selected, train_grads, (((1,), (1,)), ((), ())), preferred_element_type=jnp.float32
    )
    return (partial_scores * flags).astype(jnp.bfloat16)


def solution(mesh):
    n_dp, n_col = mesh.devices.shape
    n_x = n_col
    grid = Mesh(mesh.devices.reshape(n_x, n_dp // n_x, n_col), ("x", "zc", "col"))
    rows = ("x", "zc")
    placed = (P(rows, None), P(None, "col"), P(rows, None), P(), P())
    return jax.shard_map(
        per_device, mesh=grid, in_specs=placed, out_specs=P("col", rows), check_vma=False
    )
```

time: 76.6 us -> 71.2 us (0.930)
  other arithmetic: 2.99 us -> 0.1 us
  Pallas kernels: 61.2 us -> 59.5 us
    pallas_call x1, Pallas kernels: 61.2 us -> 59.5 us  [gather_rows(): pl.pallas_call(functools.partial(gather_kernel, n_x, n_z), out_shape=(jax...]
    reduce_or x1 -> x0, other arithmetic: 1.66 us -> none  [listed_flags(): flags = jnp.any(owned_rows == owner, axis=1)]
    reduce_sum x1 -> x0, other arithmetic: 1.32 us -> none  [listed_flags(): owner = jnp.sum(jnp.where(block_slot == dp_index, numbers, 0))]
  transfers between devices with their start and end apart: 1 -> 0, of which waited for: 0 -> 0; matrix products, arithmetic and copies ran while one was open for 4% -> 0% of each run, Pallas kernels for 0% -> 0%
where the time goes in v5:
time: 71.2 us; the launch traced here: 71 us
  Pallas kernels  59.5 us (84%)
  matrix products  5.69 us (8%)
  local copies, waits for them, and re-layouts  5.66 us (8%)
    pallas_call x1, Pallas kernels, gather_rows(): pl.pallas_call(functools.partial(gather_kernel, n_x, n_z), out_shape=(jax...  59.5 us
    dot_general x1, matrix products, per_device(): lax.dot_general(selected, train_grads, (((1,), (1,)), ((), ())), preferre...  4.6 us
    reshape x1, local copies, waits for them, and re-layouts, per_device(): held = held.reshape(n_x, 2, n_zc // 2, rows, width // 128, 128)  1.83 us
    reshape x1, local copies, waits for them, and re-layouts, per_device(): jnp.transpose(held, (2, 1, 3, 0, 4, 5)).reshape(per_col, n_x * width)  1.62 us
    unnamed x4, local copies, waits for them, and re-layouts  1.6 us

profile of v5, /device:TPU:1, one launch (start us, length us, event | category | flops | bytes accessed | tf_op | source)
XLA Modules:
  0.0 71.0 jit_solution(17041607671700288846)
XLA Ops:
  0.0 0.0 copy-start
  0.0 1.6 %copy-done = bf16[2048,512]{1,0:T(8,128)(2,1)S(1)} copy-done((bf16[2048,512]{1,0:T(8,128)(2,1)S(1)}, bf16[2048,512]{1,0:T(8,128)(2,1)}, u32[]{:S(2)}) %copy-start) | copy-done | bytes 2097176
  1.6 1.1 %convolution_convert_fusion = bf16[4,512]{1,0:T(4,128)(2,1)S(1)} fusion(bf16[4,2048]{1,0:T(4,128)(2,1)} %param.5, bf16[2048,512]{1,0:T(8,128)(2,1)S(1)} %copy-done), kind=kOutput, calls=%fused_computation.2 | convolution fusion | flops 8390656 | bytes 2117632 | tf_op jit(solution)/shard_map/dot_general | solution.py:161
  2.7 0.6 reshape.12.block_ref
  3.3 59.5 %shard_map.55 = (bf16[4,2,32,16,128]{4,3,2,1,0:T(8,128)(2,1)}, f32[256,1]{1,0:T(8,128)}) custom-call(bf16[16,128]{1,0:T(8,128)(2,1)} %reshape.12.block_ref, s32[1024,128]{1,0:T(8,128)} %cand_ref.1, s32[2,128]{1,0:T(2,128)} %bitcast.11), custom_call_target="tpu_custom_call" | custom-call | bytes 2097152 | tf_op jit(solution)/shard_map/pallas_call | solution.py:131
  62.8 0.0 copy-start.1
  62.8 1.8 %copy.8 = bf16[4,2,32,4,4,128]{5,4,0,3,1,2:T(4,128)(2,1)S(1)} copy(bf16[4,2,32,4,4,128]{5,4,3,2,1,0:T(4,128)(2,1)} %bitcast.10) | data formatting | bytes 2097152 | tf_op jit(solution)/shard_map/reshape | solution.py:165
  64.6 1.6 %reshape.15 = bf16[256,2048]{1,0:T(8,128)(2,1)} reshape(bf16[32,2,4,4,4,128]{5,4,3,2,1,0:T(4,128)(2,1)S(1)} %bitcast.9) | data formatting | bytes 2097152 | tf_op jit(solution)/shard_map/reshape | solution.py:166
  66.2 0.0 copy-done.1
  66.2 0.1 reduce
  66.4 4.6 %fusion = bf16[256,1024]{1,0:T(8,128)(2,1)} fusion(bf16[256,2048]{1,0:T(8,128)(2,1)} %reshape.15, bf16[1024,2048]{1,0:T(8,128)(2,1)} %param.7, f32[256]{0:T(256)S(1)} %reduce), kind=kOutput, calls=%fused_computation.1 | convolution fusion | flops 1074266112 | bytes 5768192 | tf_op jit(solution)/shard_map/dot_general | solution.py:167
Async XLA Ops:
  0.0 1.6 %copy-start = (bf16[2048,512]{1,0:T(8,128)(2,1)S(1)}, bf16[2048,512]{1,0:T(8,128)(2,1)}, u32[]{:S(2)}) copy-start(bf16[2048,512]{1,0:T(8,128)(2,1)} %param.6) | copy-start | bytes 6291460
  62.8 3.5 %copy-start.1 = (f32[256,1]{1,0:T(8,128)S(1)}, f32[256,1]{1,0:T(8,128)}, u32[]{:S(2)}) copy-start(f32[256,1]{1,0:T(8,128)} %get-tuple-element.8) | copy-start | bytes 3076

commit v6 on v5

--- a/solution.py
+++ b/solution.py
@@ -10,8 +10,8 @@
 MESH = pl.DeviceIdType.MESH
 
 
-def gather_kernel(n_x, n_z, block_ref, cand_ref, slot_ref, out_ref, flags_ref, held, send_z, recv_z,
-                  send_x, recv_x, send_pair, recv_pair, own_sem):
+def gather_kernel(n_x, n_z, stride, block_ref, cand_ref, slot_ref, out_ref, flags_ref, held, send_own,
+                  recv_own, send_fwd, recv_fwd, send_x, recv_x, send_pair, recv_pair, own_sem):
     me_x = lax.axis_index("x")
     me_zc = lax.axis_index("zc")
     me_y = lax.axis_index("col")
@@ -19,11 +19,22 @@
     lane = me_zc % 2
     pair = me_z * 2 + 1 - lane
     on_diagonal = me_x == me_y
-    z_peers = [(k, lax.rem(me_z + k, n_z) * 2 + lane) for k in range(1, n_z)]
+    reach = (n_z // 2, (n_z - 1) // 2)
+    near = tuple(min(stride, r) for r in reach)
     x_peers = [(k, lax.rem(me_x + k, n_x)) for k in range(1, n_x)]
 
+    def along(way, hops):
+        z = me_z + hops if way == 0 else me_z - hops
+        return lax.rem(z + 2 * n_z, n_z) * 2 + lane
+
     barrier = pltpu.get_barrier_semaphore()
-    peers = [(me_y, zc, me_x) for _, zc in z_peers] + [(px, me_zc, me_y) for _, px in x_peers]
+    peers = []
+    for way in range(2):
+        for k in range(1, near[way] + 1):
+            peers += [(me_y, along(way, k), me_x), (me_y, along(way, -k), me_x)]
+        if reach[way] > near[way]:
+            peers += [(me_x, along(way, stride), me_y), (me_x, along(way, -stride), me_y)]
+    peers += [(px, me_zc, me_y) for _, px in x_peers]
     peers.append((me_x, pair, me_y))
     for peer in peers:
         pl.semaphore_signal(barrier, inc=1, device_id=peer, device_id_type=MESH)
@@ -34,14 +45,16 @@
 
     pl.semaphore_wait(barrier, len(peers) + jnp.where(on_diagonal, 0, 1))
 
-    def z_copy(k, zc):
+    def own_copy(way, k):
         return pltpu.make_async_remote_copy(
             src_ref=block_ref, dst_ref=held.at[me_y, lane, me_z],
-            send_sem=send_z.at[k], recv_sem=recv_z.at[lax.rem(n_z - k, n_z)],
-            device_id=(me_y, zc, me_x), device_id_type=MESH)
-
-    for k, zc in z_peers:
-        z_copy(k, zc).start()
+            send_sem=send_own.at[way, k], recv_sem=recv_own.at[way, k],
+            device_id=(me_y, along(way, k), me_x), device_id_type=MESH)
+
+    for k in range(1, max(near) + 1):
+        for way in range(2):
+            if k <= near[way]:
+                own_copy(way, k).start()
     own = pltpu.make_async_copy(block_ref, held.at[me_x, lane, me_z], own_sem)
 
     @pl.when(on_diagonal)
@@ -50,7 +63,7 @@
 
     @pl.when(jnp.logical_not(on_diagonal))
     def _():
-        z_copy(0, me_zc).start()
+        own_copy(0, 0).start()
 
     rows = flags_ref.shape[0]
     slots = slot_ref[...]
@@ -60,25 +73,41 @@
     listed = cand_ref[pl.ds(pl.multiple_of(me_y * rows, rows), rows), :] == owner
     flags_ref[...] = jnp.max(listed.astype(jnp.float32), axis=1, keepdims=True)
 
-    for k in range(n_z):
-        src_z = lax.rem(me_z + k, n_z)
-        src_zc = src_z * 2 + lane
-        if k == 0:
-            @pl.when(on_diagonal)
-            def _():
-                own.wait()
-
-            @pl.when(jnp.logical_not(on_diagonal))
-            def _():
-                pltpu.make_async_remote_copy(
-                    src_ref=block_ref, dst_ref=held.at[me_x, lane, src_z],
-                    send_sem=send_z.at[0], recv_sem=recv_z.at[0],
-                    device_id=(me_y, src_zc, me_x), device_id_type=MESH).wait_recv()
-        else:
+    @pl.when(on_diagonal)
+    def _():
+        own.wait()
+
+    @pl.when(jnp.logical_not(on_diagonal))
+    def _():
+        pltpu.make_async_remote_copy(
+            src_ref=block_ref, dst_ref=held.at[me_x, lane, me_z],
+            send_sem=send_own.at[0, 0], recv_sem=recv_own.at[0, 0],
+            device_id=(me_y, me_zc, me_x), device_id_type=MESH).wait_recv()
+
+    def fwd_copy(way, hops, slot_z):
+        line = held.at[me_x, lane, slot_z]
+        return pltpu.make_async_remote_copy(
+            src_ref=line, dst_ref=line, send_sem=send_fwd.at[way, hops + stride],
+            recv_sem=recv_fwd.at[way, hops + stride],
+            device_id=(me_x, along(way, stride), me_y), device_id_type=MESH)
+
+    forwarded = []
+    for hops in range(1, max(reach) + 1):
+        for way in range(2):
+            if hops > reach[way]:
+                continue
+            origin = along(way, -hops) // 2
+            line = held.at[me_x, lane, origin]
+            if hops <= near[way]:
+                source, sems = (me_y, along(way, -hops), me_x), (send_own.at[way, hops], recv_own.at[way, hops])
+            else:
+                source, sems = (me_x, along(way, -stride), me_y), (send_fwd.at[way, hops], recv_fwd.at[way, hops])
             pltpu.make_async_remote_copy(
-                src_ref=block_ref, dst_ref=held.at[me_x, lane, src_z],
-                send_sem=send_z.at[k], recv_sem=recv_z.at[k],
-                device_id=(me_y, src_zc, me_x), device_id_type=MESH).wait_recv()
+                src_ref=line, dst_ref=line, send_sem=sems[0], recv_sem=sems[1],
+                device_id=source, device_id_type=MESH).wait_recv()
+            if hops + stride <= reach[way]:
+                fwd_copy(way, hops, origin).start()
+                forwarded.append((way, hops, origin))
 
     def to_pair(c, index):
         line = held.at[c, lane]
@@ -109,13 +138,16 @@
             src_ref=line, dst_ref=line, send_sem=send_pair.at[index], recv_sem=recv_pair.at[index],
             device_id=(me_x, pair, me_y), device_id_type=MESH).wait_recv()
 
-    for k, zc in z_peers:
-        z_copy(k, zc).wait_send()
-
-    @pl.when(jnp.logical_not(on_diagonal))
-    def _():
-        z_copy(0, me_zc).wait_send()
-
+    for way in range(2):
+        for k in range(1, near[way] + 1):
+            own_copy(way, k).wait_send()
+
+    @pl.when(jnp.logical_not(on_diagonal))
+    def _():
+        own_copy(0, 0).wait_send()
+
+    for way, hops, origin in forwarded:
+        fwd_copy(way, hops, origin).wait_send()
     for k, px in x_peers:
         x_copy(k, px).wait_send()
     to_pair(me_x, 0).wait_send()
@@ -126,10 +158,11 @@
 
 def gather_rows(block, candidates, block_slot, n_x, n_zc, rows):
     n_z = n_zc // 2
+    stride = max(1, min(4, n_z // 4))
     shape = (n_x, 2, n_z) + block.shape
     slots = block_slot.reshape(-1, 128) if block_slot.size % 128 == 0 else block_slot.reshape(1, -1)
     return pl.pallas_call(
-        functools.partial(gather_kernel, n_x, n_z),
+        functools.partial(gather_kernel, n_x, n_z, stride),
         out_shape=(
             jax.ShapeDtypeStruct(shape, block.dtype),
             jax.ShapeDtypeStruct((rows, 1), jnp.float32),
@@ -138,8 +171,10 @@
         out_specs=(pl.BlockSpec(memory_space=pltpu.VMEM), pl.BlockSpec(memory_space=pltpu.VMEM)),
         scratch_shapes=[
             pltpu.VMEM(shape, block.dtype),
-            pltpu.SemaphoreType.DMA((n_z,)),
-            pltpu.SemaphoreType.DMA((n_z,)),
+            pltpu.SemaphoreType.DMA((2, stride + 1)),
+            pltpu.SemaphoreType.DMA((2, stride + 1)),
+            pltpu.SemaphoreType.DMA((2, n_z // 2 + 1)),
+            pltpu.SemaphoreType.DMA((2, n_z // 2 + 1)),
             pltpu.SemaphoreType.DMA((n_x,)),
             pltpu.SemaphoreType.DMA((n_x,)),
             pltpu.SemaphoreType.DMA((n_x,)),

time: 71.2 us -> 68 us (0.955)
  Pallas kernels: 59.5 us -> 56.3 us
    pallas_call x1, Pallas kernels: 59.5 us -> 56.3 us  [gather_rows(): pl.pallas_call(functools.partial(gather_kernel, n_x, n_z, stride), out_sh...]
where the time goes in v6:
time: 68 us; the launch traced here: 67.7 us
  Pallas kernels  56.3 us (83%)
  matrix products  5.69 us (8%)
  local copies, waits for them, and re-layouts  5.66 us (8%)
    pallas_call x1, Pallas kernels, gather_rows(): pl.pallas_call(functools.partial(gather_kernel, n_x, n_z, stride), out_sh...  56.3 us
    dot_general x1, matrix products, per_device(): lax.dot_general(selected, train_grads, (((1,), (1,)), ((), ())), preferre...  4.6 us
    reshape x1, local copies, waits for them, and re-layouts, per_device(): held = held.reshape(n_x, 2, n_zc // 2, rows, width // 128, 128)  1.83 us
    reshape x1, local copies, waits for them, and re-layouts, per_device(): jnp.transpose(held, (2, 1, 3, 0, 4, 5)).reshape(per_col, n_x * width)  1.62 us
    unnamed x4, local copies, waits for them, and re-layouts  1.6 us

profile of v6, /device:TPU:1, one launch (start us, length us, event | category | flops | bytes accessed | tf_op | source)
XLA Modules:
  0.0 67.7 jit_solution(11091235087230845241)
XLA Ops:
  0.0 0.0 copy-start
  0.0 1.6 %copy-done = bf16[2048,512]{1,0:T(8,128)(2,1)S(1)} copy-done((bf16[2048,512]{1,0:T(8,128)(2,1)S(1)}, bf16[2048,512]{1,0:T(8,128)(2,1)}, u32[]{:S(2)}) %copy-start) | copy-done | bytes 2097176
  1.6 1.1 %convolution_convert_fusion = bf16[4,512]{1,0:T(4,128)(2,1)S(1)} fusion(bf16[4,2048]{1,0:T(4,128)(2,1)} %param.5, bf16[2048,512]{1,0:T(8,128)(2,1)S(1)} %copy-done), kind=kOutput, calls=%fused_computation.2 | convolution fusion | flops 8390656 | bytes 2117632 | tf_op jit(solution)/shard_map/dot_general | solution.py:196
  2.7 0.6 reshape.12.block_ref
  3.3 56.3 %shard_map.55 = (bf16[4,2,32,16,128]{4,3,2,1,0:T(8,128)(2,1)}, f32[256,1]{1,0:T(8,128)}) custom-call(bf16[16,128]{1,0:T(8,128)(2,1)} %reshape.12.block_ref, s32[1024,128]{1,0:T(8,128)} %cand_ref.1, s32[2,128]{1,0:T(2,128)} %bitcast.11), custom_call_target="tpu_custom_call" | custom-call | bytes 2097152 | tf_op jit(solution)/shard_map/pallas_call | solution.py:164
  59.6 0.0 copy-start.1
  59.6 1.8 %copy.8 = bf16[4,2,32,4,4,128]{5,4,0,3,1,2:T(4,128)(2,1)S(1)} copy(bf16[4,2,32,4,4,128]{5,4,3,2,1,0:T(4,128)(2,1)} %bitcast.10) | data formatting | bytes 2097152 | tf_op jit(solution)/shard_map/reshape | solution.py:200
  61.4 1.6 %reshape.15 = bf16[256,2048]{1,0:T(8,128)(2,1)} reshape(bf16[32,2,4,4,4,128]{5,4,3,2,1,0:T(4,128)(2,1)S(1)} %bitcast.9) | data formatting | bytes 2097152 | tf_op jit(solution)/shard_map/reshape | solution.py:201
  63.0 0.0 copy-done.1
  63.0 0.1 reduce
  63.1 4.6 %fusion = bf16[256,1024]{1,0:T(8,128)(2,1)} fusion(bf16[256,2048]{1,0:T(8,128)(2,1)} %reshape.15, bf16[1024,2048]{1,0:T(8,128)(2,1)} %param.7, f32[256]{0:T(256)S(1)} %reduce), kind=kOutput, calls=%fused_computation.1 | convolution fusion | flops 1074266112 | bytes 5768192 | tf_op jit(solution)/shard_map/dot_general | solution.py:202
Async XLA Ops:
  0.0 1.6 %copy-start = (bf16[2048,512]{1,0:T(8,128)(2,1)S(1)}, bf16[2048,512]{1,0:T(8,128)(2,1)}, u32[]{:S(2)}) copy-start(bf16[2048,512]{1,0:T(8,128)(2,1)} %param.6) | copy-start | bytes 6291460
  59.6 3.5 %copy-start.1 = (f32[256,1]{1,0:T(8,128)S(1)}, f32[256,1]{1,0:T(8,128)}, u32[]{:S(2)}) copy-start(f32[256,1]{1,0:T(8,128)} %get-tuple-element.8) | copy-start | bytes 3076

commit v7 on v6

--- a/solution.py
+++ b/solution.py
@@ -34,7 +34,7 @@
             peers += [(me_y, along(way, k), me_x), (me_y, along(way, -k), me_x)]
         if reach[way] > near[way]:
             peers += [(me_x, along(way, stride), me_y), (me_x, along(way, -stride), me_y)]
-    peers += [(px, me_zc, me_y) for _, px in x_peers]
+    peers += [(px, me_z * 2 + other, me_y) for _, px in x_peers for other in range(2)]
     peers.append((me_x, pair, me_y))
     for peer in peers:
         pl.semaphore_signal(barrier, inc=1, device_id=peer, device_id_type=MESH)
@@ -73,6 +73,18 @@
     listed = cand_ref[pl.ds(pl.multiple_of(me_y * rows, rows), rows), :] == owner
     flags_ref[...] = jnp.max(listed.astype(jnp.float32), axis=1, keepdims=True)
 
+    def spread(slot_z):
+        line = held.at[me_x, lane, slot_z]
+        pltpu.make_async_remote_copy(
+            src_ref=line, dst_ref=line, send_sem=send_pair, recv_sem=recv_pair,
+            device_id=(me_x, pair, me_y), device_id_type=MESH).start()
+        for k, px in x_peers:
+            for other in range(2):
+                pltpu.make_async_remote_copy(
+                    src_ref=line, dst_ref=line, send_sem=send_x.at[k, other],
+                    recv_sem=recv_x.at[n_x - k, lane],
+                    device_id=(px, me_z * 2 + other, me_y), device_id_type=MESH).start()
+
     @pl.when(on_diagonal)
     def _():
         own.wait()
@@ -83,6 +95,8 @@
             src_ref=block_ref, dst_ref=held.at[me_x, lane, me_z],
             send_sem=send_own.at[0, 0], recv_sem=recv_own.at[0, 0],
             device_id=(me_y, me_zc, me_x), device_id_type=MESH).wait_recv()
+
+    spread(me_z)
 
     def fwd_copy(way, hops, slot_z):
         line = held.at[me_x, lane, slot_z]
@@ -108,35 +122,19 @@
             if hops + stride <= reach[way]:
                 fwd_copy(way, hops, origin).start()
                 forwarded.append((way, hops, origin))
-
-    def to_pair(c, index):
-        line = held.at[c, lane]
-        return pltpu.make_async_remote_copy(
-            src_ref=line, dst_ref=line, send_sem=send_pair.at[index], recv_sem=recv_pair.at[index],
-            device_id=(me_x, pair, me_y), device_id_type=MESH)
-
-    def x_copy(k, px):
-        line = held.at[me_x, lane]
-        return pltpu.make_async_remote_copy(
-            src_ref=line, dst_ref=line, send_sem=send_x.at[k], recv_sem=recv_x.at[n_x - k],
-            device_id=(px, me_zc, me_y), device_id_type=MESH)
-
-    to_pair(me_x, 0).start()
-    for k, px in x_peers:
-        x_copy(k, px).start()
-    for k, px in x_peers:
-        line = held.at[px, lane]
-        pltpu.make_async_remote_copy(
-            src_ref=line, dst_ref=line, send_sem=send_x.at[k], recv_sem=recv_x.at[k],
-            device_id=(px, me_zc, me_y), device_id_type=MESH).wait_recv()
-        to_pair(px, k).start()
-
-    for index in range(n_x):
-        c = me_x if index == 0 else x_peers[index - 1][1]
-        line = held.at[c, 1 - lane]
-        pltpu.make_async_remote_copy(
-            src_ref=line, dst_ref=line, send_sem=send_pair.at[index], recv_sem=recv_pair.at[index],
-            device_id=(me_x, pair, me_y), device_id_type=MESH).wait_recv()
+            spread(origin)
+
+    for other_lane in range(2):
+        for k, px in x_peers:
+            line = held.at[px, other_lane]
+            pltpu.make_async_remote_copy(
+                src_ref=line, dst_ref=line, send_sem=send_x.at[k, other_lane],
+                recv_sem=recv_x.at[k, other_lane],
+                device_id=(px, me_z * 2 + other_lane, me_y), device_id_type=MESH).wait()
+    line = held.at[me_x, 1 - lane]
+    pltpu.make_async_remote_copy(
+        src_ref=line, dst_ref=line, send_sem=send_pair, recv_sem=recv_pair,
+        device_id=(me_x, pair, me_y), device_id_type=MESH).wait()
 
     for way in range(2):
         for k in range(1, near[way] + 1):
@@ -148,11 +146,6 @@
 
     for way, hops, origin in forwarded:
         fwd_copy(way, hops, origin).wait_send()
-    for k, px in x_peers:
-        x_copy(k, px).wait_send()
-    to_pair(me_x, 0).wait_send()
-    for k, px in x_peers:
-        to_pair(px, k).wait_send()
     out_ref[...] = held[...]
 
 
@@ -175,10 +168,10 @@
             pltpu.SemaphoreType.DMA((2, stride + 1)),
             pltpu.SemaphoreType.DMA((2, n_z // 2 + 1)),
             pltpu.SemaphoreType.DMA((2, n_z // 2 + 1)),
-            pltpu.SemaphoreType.DMA((n_x,)),
-            pltpu.SemaphoreType.DMA((n_x,)),
-            pltpu.SemaphoreType.DMA((n_x,)),
-            pltpu.SemaphoreType.DMA((n_x,)),
+            pltpu.SemaphoreType.DMA((n_x, 2)),
+            pltpu.SemaphoreType.DMA((n_x, 2)),
+            pltpu.SemaphoreType.DMA(()),
+            pltpu.SemaphoreType.DMA(()),
             pltpu.SemaphoreType.DMA(()),
         ],
         compiler_params=pltpu.CompilerParams(collective_id=0, has_side_effects=True),

time: 68 us -> 63.9 us (0.940)
  Pallas kernels: 56.3 us -> 52.2 us
    pallas_call x1, Pallas kernels: 56.3 us -> 52.2 us  [gather_rows(): pl.pallas_call(functools.partial(gather_kernel, n_x, n_z, stride), out_sh...]
where the time goes in v7:
time: 63.9 us; the launch traced here: 63.6 us
  Pallas kernels  52.2 us (82%)
  matrix products  5.69 us (9%)
  local copies, waits for them, and re-layouts  5.66 us (9%)
    pallas_call x1, Pallas kernels, gather_rows(): pl.pallas_call(functools.partial(gather_kernel, n_x, n_z, stride), out_sh...  52.2 us
    dot_general x1, matrix products, per_device(): lax.dot_general(selected, train_grads, (((1,), (1,)), ((), ())), preferre...  4.6 us
    reshape x1, local copies, waits for them, and re-layouts, per_device(): held = held.reshape(n_x, 2, n_zc // 2, rows, width // 128, 128)  1.83 us
    reshape x1, local copies, waits for them, and re-layouts, per_device(): jnp.transpose(held, (2, 1, 3, 0, 4, 5)).reshape(per_col, n_x * width)  1.62 us
    unnamed x4, local copies, waits for them, and re-layouts  1.6 us

profile of v7, /device:TPU:1, one launch (start us, length us, event | category | flops | bytes accessed | tf_op | source)
XLA Modules:
  0.0 63.6 jit_solution(14641323484013616308)
XLA Ops:
  0.0 0.0 copy-start
  0.0 1.6 %copy-done = bf16[2048,512]{1,0:T(8,128)(2,1)S(1)} copy-done((bf16[2048,512]{1,0:T(8,128)(2,1)S(1)}, bf16[2048,512]{1,0:T(8,128)(2,1)}, u32[]{:S(2)}) %copy-start) | copy-done | bytes 2097176
  1.6 1.1 %convolution_convert_fusion = bf16[4,512]{1,0:T(4,128)(2,1)S(1)} fusion(bf16[4,2048]{1,0:T(4,128)(2,1)} %param.5, bf16[2048,512]{1,0:T(8,128)(2,1)S(1)} %copy-done), kind=kOutput, calls=%fused_computation.2 | convolution fusion | flops 8390656 | bytes 2117632 | tf_op jit(solution)/shard_map/dot_general | solution.py:189
  2.7 0.6 reshape.12.block_ref
  3.3 52.2 %shard_map.55 = (bf16[4,2,32,16,128]{4,3,2,1,0:T(8,128)(2,1)}, f32[256,1]{1,0:T(8,128)}) custom-call(bf16[16,128]{1,0:T(8,128)(2,1)} %reshape.12.block_ref, s32[1024,128]{1,0:T(8,128)} %cand_ref.1, s32[2,128]{1,0:T(2,128)} %bitcast.11), custom_call_target="tpu_custom_call" | custom-call | bytes 2097152 | tf_op jit(solution)/shard_map/pallas_call | solution.py:157
  55.5 0.0 copy-start.1
  55.5 1.8 %copy.8 = bf16[4,2,32,4,4,128]{5,4,0,3,1,2:T(4,128)(2,1)S(1)} copy(bf16[4,2,32,4,4,128]{5,4,3,2,1,0:T(4,128)(2,1)} %bitcast.10) | data formatting | bytes 2097152 | tf_op jit(solution)/shard_map/reshape | solution.py:193
  57.3 1.6 %reshape.15 = bf16[256,2048]{1,0:T(8,128)(2,1)} reshape(bf16[32,2,4,4,4,128]{5,4,3,2,1,0:T(4,128)(2,1)S(1)} %bitcast.9) | data formatting | bytes 2097152 | tf_op jit(solution)/shard_map/reshape | solution.py:194
  58.9 0.0 copy-done.1
  58.9 0.1 reduce
  59.0 4.6 %fusion = bf16[256,1024]{1,0:T(8,128)(2,1)} fusion(bf16[256,2048]{1,0:T(8,128)(2,1)} %reshape.15, bf16[1024,2048]{1,0:T(8,128)(2,1)} %param.7, f32[256]{0:T(256)S(1)} %reduce), kind=kOutput, calls=%fused_computation.1 | convolution fusion | flops 1074266112 | bytes 5768192 | tf_op jit(solution)/shard_map/dot_general | solution.py:195
Async XLA Ops:
  0.0 1.6 %copy-start = (bf16[2048,512]{1,0:T(8,128)(2,1)S(1)}, bf16[2048,512]{1,0:T(8,128)(2,1)}, u32[]{:S(2)}) copy-start(bf16[2048,512]{1,0:T(8,128)(2,1)} %param.6) | copy-start | bytes 6291460
  55.5 3.5 %copy-start.1 = (f32[256,1]{1,0:T(8,128)S(1)}, f32[256,1]{1,0:T(8,128)}, u32[]{:S(2)}) copy-start(f32[256,1]{1,0:T(8,128)} %get-tuple-element.8) | copy-start | bytes 3076

commit v8 on v7

--- a/solution.py
+++ b/solution.py
@@ -151,7 +151,7 @@
 
 def gather_rows(block, candidates, block_slot, n_x, n_zc, rows):
     n_z = n_zc // 2
-    stride = max(1, min(4, n_z // 4))
+    stride = max(1, min(8, n_z // 4))
     shape = (n_x, 2, n_z) + block.shape
     slots = block_slot.reshape(-1, 128) if block_slot.size % 128 == 0 else block_slot.reshape(1, -1)
     return pl.pallas_call(

time: 63.9 us -> 62.3 us (0.975)
  Pallas kernels: 52.2 us -> 50.6 us
    pallas_call x1, Pallas kernels: 52.2 us -> 50.6 us  [gather_rows(): pl.pallas_call(functools.partial(gather_kernel, n_x, n_z, stride), out_sh...]
where the time goes in v8:
time: 62.3 us; the launch traced here: 62 us
  Pallas kernels  50.6 us (81%)
  matrix products  5.69 us (9%)
  local copies, waits for them, and re-layouts  5.66 us (9%)
    pallas_call x1, Pallas kernels, gather_rows(): pl.pallas_call(functools.partial(gather_kernel, n_x, n_z, stride), out_sh...  50.6 us
    dot_general x1, matrix products, per_device(): lax.dot_general(selected, train_grads, (((1,), (1,)), ((), ())), preferre...  4.6 us
    reshape x1, local copies, waits for them, and re-layouts, per_device(): held = held.reshape(n_x, 2, n_zc // 2, rows, width // 128, 128)  1.83 us
    reshape x1, local copies, waits for them, and re-layouts, per_device(): jnp.transpose(held, (2, 1, 3, 0, 4, 5)).reshape(per_col, n_x * width)  1.62 us
    unnamed x4, local copies, waits for them, and re-layouts  1.6 us

profile of v8, /device:TPU:1, one launch (start us, length us, event | category | flops | bytes accessed | tf_op | source)
XLA Modules:
  0.0 62.0 jit_solution(4115698417662471892)
XLA Ops:
  0.0 0.0 copy-start
  0.0 1.6 %copy-done = bf16[2048,512]{1,0:T(8,128)(2,1)S(1)} copy-done((bf16[2048,512]{1,0:T(8,128)(2,1)S(1)}, bf16[2048,512]{1,0:T(8,128)(2,1)}, u32[]{:S(2)}) %copy-start) | copy-done | bytes 2097176
  1.6 1.1 %convolution_convert_fusion = bf16[4,512]{1,0:T(4,128)(2,1)S(1)} fusion(bf16[4,2048]{1,0:T(4,128)(2,1)} %param.5, bf16[2048,512]{1,0:T(8,128)(2,1)S(1)} %copy-done), kind=kOutput, calls=%fused_computation.2 | convolution fusion | flops 8390656 | bytes 2117632 | tf_op jit(solution)/shard_map/dot_general | solution.py:189
  2.7 0.6 reshape.12.block_ref
  3.3 50.6 %shard_map.55 = (bf16[4,2,32,16,128]{4,3,2,1,0:T(8,128)(2,1)}, f32[256,1]{1,0:T(8,128)}) custom-call(bf16[16,128]{1,0:T(8,128)(2,1)} %reshape.12.block_ref, s32[1024,128]{1,0:T(8,128)} %cand_ref.1, s32[2,128]{1,0:T(2,128)} %bitcast.11), custom_call_target="tpu_custom_call" | custom-call | bytes 2097152 | tf_op jit(solution)/shard_map/pallas_call | solution.py:157
  53.9 0.0 copy-start.1
  53.9 1.8 %copy.8 = bf16[4,2,32,4,4,128]{5,4,0,3,1,2:T(4,128)(2,1)S(1)} copy(bf16[4,2,32,4,4,128]{5,4,3,2,1,0:T(4,128)(2,1)} %bitcast.10) | data formatting | bytes 2097152 | tf_op jit(solution)/shard_map/reshape | solution.py:193
  55.7 1.6 %reshape.15 = bf16[256,2048]{1,0:T(8,128)(2,1)} reshape(bf16[32,2,4,4,4,128]{5,4,3,2,1,0:T(4,128)(2,1)S(1)} %bitcast.9) | data formatting | bytes 2097152 | tf_op jit(solution)/shard_map/reshape | solution.py:194
  57.3 0.0 copy-done.1
  57.3 0.1 reduce
  57.4 4.6 %fusion = bf16[256,1024]{1,0:T(8,128)(2,1)} fusion(bf16[256,2048]{1,0:T(8,128)(2,1)} %reshape.15, bf16[1024,2048]{1,0:T(8,128)(2,1)} %param.7, f32[256]{0:T(256)S(1)} %reduce), kind=kOutput, calls=%fused_computation.1 | convolution fusion | flops 1074266112 | bytes 5768192 | tf_op jit(solution)/shard_map/dot_general | solution.py:195
Async XLA Ops:
  0.0 1.6 %copy-start = (bf16[2048,512]{1,0:T(8,128)(2,1)S(1)}, bf16[2048,512]{1,0:T(8,128)(2,1)}, u32[]{:S(2)}) copy-start(bf16[2048,512]{1,0:T(8,128)(2,1)} %param.6) | copy-start | bytes 6291460
  53.9 3.5 %copy-start.1 = (f32[256,1]{1,0:T(8,128)S(1)}, f32[256,1]{1,0:T(8,128)}, u32[]{:S(2)}) copy-start(f32[256,1]{1,0:T(8,128)} %get-tuple-element.8) | copy-start | bytes 3076

commit v9 on v8

--- a/solution.py
+++ b/solution.py
@@ -11,7 +11,8 @@
 
 
 def gather_kernel(n_x, n_z, stride, block_ref, cand_ref, slot_ref, out_ref, flags_ref, held, send_own,
-                  recv_own, send_fwd, recv_fwd, send_x, recv_x, send_pair, recv_pair, own_sem):
+                  recv_own, send_fwd, recv_fwd, send_x, recv_x, send_pair, recv_pair, send_fp, recv_fp,
+                  own_sem):
     me_x = lax.axis_index("x")
     me_zc = lax.axis_index("zc")
     me_y = lax.axis_index("col")
@@ -34,7 +35,7 @@
             peers += [(me_y, along(way, k), me_x), (me_y, along(way, -k), me_x)]
         if reach[way] > near[way]:
             peers += [(me_x, along(way, stride), me_y), (me_x, along(way, -stride), me_y)]
-    peers += [(px, me_z * 2 + other, me_y) for _, px in x_peers for other in range(2)]
+    peers += [(px, me_zc, me_y) for _, px in x_peers]
     peers.append((me_x, pair, me_y))
     for peer in peers:
         pl.semaphore_signal(barrier, inc=1, device_id=peer, device_id_type=MESH)
@@ -79,11 +80,10 @@
             src_ref=line, dst_ref=line, send_sem=send_pair, recv_sem=recv_pair,
             device_id=(me_x, pair, me_y), device_id_type=MESH).start()
         for k, px in x_peers:
-            for other in range(2):
-                pltpu.make_async_remote_copy(
-                    src_ref=line, dst_ref=line, send_sem=send_x.at[k, other],
-                    recv_sem=recv_x.at[n_x - k, lane],
-                    device_id=(px, me_z * 2 + other, me_y), device_id_type=MESH).start()
+            pltpu.make_async_remote_copy(
+                src_ref=line, dst_ref=line, send_sem=send_x.at[k],
+                recv_sem=recv_x.at[n_x - k, slot_z],
+                device_id=(px, me_zc, me_y), device_id_type=MESH).start()
 
     @pl.when(on_diagonal)
     def _():
@@ -106,6 +106,7 @@
             device_id=(me_x, along(way, stride), me_y), device_id_type=MESH)
 
     forwarded = []
+    origins = [me_z]
     for hops in range(1, max(reach) + 1):
         for way in range(2):
             if hops > reach[way]:
@@ -123,14 +124,26 @@
                 fwd_copy(way, hops, origin).start()
                 forwarded.append((way, hops, origin))
             spread(origin)
-
-    for other_lane in range(2):
+            origins.append(origin)
+
+    for origin in origins:
         for k, px in x_peers:
-            line = held.at[px, other_lane]
-            pltpu.make_async_remote_copy(
-                src_ref=line, dst_ref=line, send_sem=send_x.at[k, other_lane],
-                recv_sem=recv_x.at[k, other_lane],
-                device_id=(px, me_z * 2 + other_lane, me_y), device_id_type=MESH).wait()
+            line = held.at[px, lane, origin]
+            pltpu.make_async_remote_copy(
+                src_ref=line, dst_ref=line, send_sem=send_x.at[k], recv_sem=recv_x.at[k, origin],
+                device_id=(px, me_zc, me_y), device_id_type=MESH).wait_recv()
+            pltpu.make_async_remote_copy(
+                src_ref=line, dst_ref=line, send_sem=send_fp.at[k], recv_sem=recv_fp.at[k],
+                device_id=(me_x, pair, me_y), device_id_type=MESH).start()
+    for k, px in x_peers:
+        line = held.at[px, 1 - lane]
+        pltpu.make_async_remote_copy(
+            src_ref=line, dst_ref=line, send_sem=send_fp.at[k], recv_sem=recv_fp.at[k],
+            device_id=(me_x, pair, me_y), device_id_type=MESH).wait()
+        line = held.at[me_x, lane]
+        pltpu.make_async_remote_copy(
+            src_ref=line, dst_ref=line, send_sem=send_x.at[k], recv_sem=recv_x.at[n_x - k, 0],
+            device_id=(px, me_zc, me_y), device_id_type=MESH).wait_send()
     line = held.at[me_x, 1 - lane]
     pltpu.make_async_remote_copy(
         src_ref=line, dst_ref=line, send_sem=send_pair, recv_sem=recv_pair,
@@ -168,10 +181,12 @@
             pltpu.SemaphoreType.DMA((2, stride + 1)),
             pltpu.SemaphoreType.DMA((2, n_z // 2 + 1)),
             pltpu.SemaphoreType.DMA((2, n_z // 2 + 1)),
-            pltpu.SemaphoreType.DMA((n_x, 2)),
-            pltpu.SemaphoreType.DMA((n_x, 2)),
+            pltpu.SemaphoreType.DMA((n_x,)),
+            pltpu.SemaphoreType.DMA((n_x, n_z)),
             pltpu.SemaphoreType.DMA(()),
             pltpu.SemaphoreType.DMA(()),
+            pltpu.SemaphoreType.DMA((n_x,)),
+            pltpu.SemaphoreType.DMA((n_x,)),
             pltpu.SemaphoreType.DMA(()),
         ],
         compiler_params=pltpu.CompilerParams(collective_id=0, has_side_effects=True),

time: 62.3 us -> 64.3 us (1.032)
  Pallas kernels: 50.6 us -> 52.5 us
    pallas_call x1, Pallas kernels: 50.6 us -> 52.5 us  [gather_rows(): pl.pallas_call(functools.partial(gather_kernel, n_x, n_z, stride), out_sh...]
where the time goes in v9:
time: 64.3 us; the launch traced here: 64 us
  Pallas kernels  52.5 us (82%)
  matrix products  5.68 us (9%)
  local copies, waits for them, and re-layouts  5.66 us (9%)
    pallas_call x1, Pallas kernels, gather_rows(): pl.pallas_call(functools.partial(gather_kernel, n_x, n_z, stride), out_sh...  52.5 us
    dot_general x1, matrix products, per_device(): lax.dot_general(selected, train_grads, (((1,), (1,)), ((), ())), preferre...  4.6 us
    reshape x1, local copies, waits for them, and re-layouts, per_device(): held = held.reshape(n_x, 2, n_zc // 2, rows, width // 128, 128)  1.83 us
    reshape x1, local copies, waits for them, and re-layouts, per_device(): jnp.transpose(held, (2, 1, 3, 0, 4, 5)).reshape(per_col, n_x * width)  1.62 us
    unnamed x4, local copies, waits for them, and re-layouts  1.6 us

profile of v9, /device:TPU:1, one launch (start us, length us, event | category | flops | bytes accessed | tf_op | source)
XLA Modules:
  0.0 64.0 jit_solution(11406963982711080572)
XLA Ops:
  0.0 0.0 copy-start
  0.0 1.6 %copy-done = bf16[2048,512]{1,0:T(8,128)(2,1)S(1)} copy-done((bf16[2048,512]{1,0:T(8,128)(2,1)S(1)}, bf16[2048,512]{1,0:T(8,128)(2,1)}, u32[]{:S(2)}) %copy-start) | copy-done | bytes 2097176
  1.6 1.1 %convolution_convert_fusion = bf16[4,512]{1,0:T(4,128)(2,1)S(1)} fusion(bf16[4,2048]{1,0:T(4,128)(2,1)} %param.5, bf16[2048,512]{1,0:T(8,128)(2,1)S(1)} %copy-done), kind=kOutput, calls=%fused_computation.2 | convolution fusion | flops 8390656 | bytes 2117632 | tf_op jit(solution)/shard_map/dot_general | solution.py:204
  2.7 0.6 reshape.12.block_ref
  3.3 52.5 %shard_map.55 = (bf16[4,2,32,16,128]{4,3,2,1,0:T(8,128)(2,1)}, f32[256,1]{1,0:T(8,128)}) custom-call(bf16[16,128]{1,0:T(8,128)(2,1)} %reshape.12.block_ref, s32[1024,128]{1,0:T(8,128)} %cand_ref.1, s32[2,128]{1,0:T(2,128)} %bitcast.11), custom_call_target="tpu_custom_call" | custom-call | bytes 2097152 | tf_op jit(solution)/shard_map/pallas_call | solution.py:170
  55.8 0.0 copy-start.1
  55.8 1.8 %copy.8 = bf16[4,2,32,4,4,128]{5,4,0,3,1,2:T(4,128)(2,1)S(1)} copy(bf16[4,2,32,4,4,128]{5,4,3,2,1,0:T(4,128)(2,1)} %bitcast.10) | data formatting | bytes 2097152 | tf_op jit(solution)/shard_map/reshape | solution.py:208
  57.7 1.6 %reshape.15 = bf16[256,2048]{1,0:T(8,128)(2,1)} reshape(bf16[32,2,4,4,4,128]{5,4,3,2,1,0:T(4,128)(2,1)S(1)} %bitcast.9) | data formatting | bytes 2097152 | tf_op jit(solution)/shard_map/reshape | solution.py:209
  59.3 0.0 copy-done.1
  59.3 0.1 reduce
  59.4 4.6 %fusion = bf16[256,1024]{1,0:T(8,128)(2,1)} fusion(bf16[256,2048]{1,0:T(8,128)(2,1)} %reshape.15, bf16[1024,2048]{1,0:T(8,128)(2,1)} %param.7, f32[256]{0:T(256)S(1)} %reduce), kind=kOutput, calls=%fused_computation.1 | convolution fusion | flops 1074266112 | bytes 5768192 | tf_op jit(solution)/shard_map/dot_general | solution.py:210
Async XLA Ops:
  0.0 1.6 %copy-start = (bf16[2048,512]{1,0:T(8,128)(2,1)S(1)}, bf16[2048,512]{1,0:T(8,128)(2,1)}, u32[]{:S(2)}) copy-start(bf16[2048,512]{1,0:T(8,128)(2,1)} %param.6) | copy-start | bytes 6291460
  55.8 3.5 %copy-start.1 = (f32[256,1]{1,0:T(8,128)S(1)}, f32[256,1]{1,0:T(8,128)}, u32[]{:S(2)}) copy-start(f32[256,1]{1,0:T(8,128)} %get-tuple-element.8) | copy-start | bytes 3076

commit v10 on v8

--- a/solution.py
+++ b/solution.py
@@ -10,7 +10,7 @@
 MESH = pl.DeviceIdType.MESH
 
 
-def gather_kernel(n_x, n_z, stride, block_ref, cand_ref, slot_ref, out_ref, flags_ref, held, send_own,
+def gather_kernel(n_x, n_z, stride, block_ref, cand_ref, slot_ref, held, flags_ref, send_own,
                   recv_own, send_fwd, recv_fwd, send_x, recv_x, send_pair, recv_pair, own_sem):
     me_x = lax.axis_index("x")
     me_zc = lax.axis_index("zc")
@@ -146,7 +146,6 @@
 
     for way, hops, origin in forwarded:
         fwd_copy(way, hops, origin).wait_send()
-    out_ref[...] = held[...]
 
 
 def gather_rows(block, candidates, block_slot, n_x, n_zc, rows):
@@ -163,7 +162,6 @@
         in_specs=[pl.BlockSpec(memory_space=pltpu.VMEM)] * 3,
         out_specs=(pl.BlockSpec(memory_space=pltpu.VMEM), pl.BlockSpec(memory_space=pltpu.VMEM)),
         scratch_shapes=[
-            pltpu.VMEM(shape, block.dtype),
             pltpu.SemaphoreType.DMA((2, stride + 1)),
             pltpu.SemaphoreType.DMA((2, stride + 1)),
             pltpu.SemaphoreType.DMA((2, n_z // 2 + 1)),

time: 62.3 us -> 62.3 us (level)
  no operation moved by 1% of the time
where the time goes in v10:
time: 62.3 us; the launch traced here: 62 us
  Pallas kernels  50.5 us (81%)
  matrix products  5.68 us (9%)
  local copies, waits for them, and re-layouts  5.66 us (9%)
    pallas_call x1, Pallas kernels, gather_rows(): pl.pallas_call(functools.partial(gather_kernel, n_x, n_z, stride), out_sh...  50.5 us
    dot_general x1, matrix products, per_device(): lax.dot_general(selected, train_grads, (((1,), (1,)), ((), ())), preferre...  4.6 us
    reshape x1, local copies, waits for them, and re-layouts, per_device(): held = held.reshape(n_x, 2, n_zc // 2, rows, width // 128, 128)  1.83 us
    reshape x1, local copies, waits for them, and re-layouts, per_device(): jnp.transpose(held, (2, 1, 3, 0, 4, 5)).reshape(per_col, n_x * width)  1.62 us
    unnamed x4, local copies, waits for them, and re-layouts  1.6 us

profile of v10, /device:TPU:1, one launch (start us, length us, event | category | flops | bytes accessed | tf_op | source)
XLA Modules:
  0.0 62.0 jit_solution(3583191349042970212)
XLA Ops:
  0.0 0.0 copy-start
  0.0 1.6 %copy-done = bf16[2048,512]{1,0:T(8,128)(2,1)S(1)} copy-done((bf16[2048,512]{1,0:T(8,128)(2,1)S(1)}, bf16[2048,512]{1,0:T(8,128)(2,1)}, u32[]{:S(2)}) %copy-start) | copy-done | bytes 2097176
  1.6 1.1 %convolution_convert_fusion = bf16[4,512]{1,0:T(4,128)(2,1)S(1)} fusion(bf16[4,2048]{1,0:T(4,128)(2,1)} %param.5, bf16[2048,512]{1,0:T(8,128)(2,1)S(1)} %copy-done), kind=kOutput, calls=%fused_computation.2 | convolution fusion | flops 8390656 | bytes 2117632 | tf_op jit(solution)/shard_map/dot_general | solution.py:187
  2.7 0.6 reshape.12.block_ref
  3.3 50.5 %shard_map.55 = (bf16[4,2,32,16,128]{4,3,2,1,0:T(8,128)(2,1)}, f32[256,1]{1,0:T(8,128)}) custom-call(bf16[16,128]{1,0:T(8,128)(2,1)} %reshape.12.block_ref, s32[1024,128]{1,0:T(8,128)} %cand_ref.1, s32[2,128]{1,0:T(2,128)} %bitcast.11), custom_call_target="tpu_custom_call" | custom-call | bytes 2097152 | tf_op jit(solution)/shard_map/pallas_call | solution.py:156
  53.8 0.0 copy-start.1
  53.8 1.8 %copy.8 = bf16[4,2,32,4,4,128]{5,4,0,3,1,2:T(4,128)(2,1)S(1)} copy(bf16[4,2,32,4,4,128]{5,4,3,2,1,0:T(4,128)(2,1)} %bitcast.10) | data formatting | bytes 2097152 | tf_op jit(solution)/shard_map/reshape | solution.py:191
  55.7 1.6 %reshape.15 = bf16[256,2048]{1,0:T(8,128)(2,1)} reshape(bf16[32,2,4,4,4,128]{5,4,3,2,1,0:T(4,128)(2,1)S(1)} %bitcast.9) | data formatting | bytes 2097152 | tf_op jit(solution)/shard_map/reshape | solution.py:192
  57.3 0.0 copy-done.1
  57.3 0.1 reduce
  57.4 4.6 %fusion = bf16[256,1024]{1,0:T(8,128)(2,1)} fusion(bf16[256,2048]{1,0:T(8,128)(2,1)} %reshape.15, bf16[1024,2048]{1,0:T(8,128)(2,1)} %param.7, f32[256]{0:T(256)S(1)} %reduce), kind=kOutput, calls=%fused_computation.1 | convolution fusion | flops 1074266112 | bytes 5768192 | tf_op jit(solution)/shard_map/dot_general | solution.py:193
Async XLA Ops:
  0.0 1.6 %copy-start = (bf16[2048,512]{1,0:T(8,128)(2,1)S(1)}, bf16[2048,512]{1,0:T(8,128)(2,1)}, u32[]{:S(2)}) copy-start(bf16[2048,512]{1,0:T(8,128)(2,1)} %param.6) | copy-start | bytes 6291460
  53.8 3.5 %copy-start.1 = (f32[256,1]{1,0:T(8,128)S(1)}, f32[256,1]{1,0:T(8,128)}, u32[]{:S(2)}) copy-start(f32[256,1]{1,0:T(8,128)} %get-tuple-element.8) | copy-start | bytes 3076

commit v11 on v10

--- a/solution.py
+++ b/solution.py
@@ -75,15 +75,15 @@
 
     def spread(slot_z):
         line = held.at[me_x, lane, slot_z]
-        pltpu.make_async_remote_copy(
-            src_ref=line, dst_ref=line, send_sem=send_pair, recv_sem=recv_pair,
-            device_id=(me_x, pair, me_y), device_id_type=MESH).start()
         for k, px in x_peers:
             for other in range(2):
                 pltpu.make_async_remote_copy(
                     src_ref=line, dst_ref=line, send_sem=send_x.at[k, other],
                     recv_sem=recv_x.at[n_x - k, lane],
                     device_id=(px, me_z * 2 + other, me_y), device_id_type=MESH).start()
+        pltpu.make_async_remote_copy(
+            src_ref=line, dst_ref=line, send_sem=send_pair, recv_sem=recv_pair,
+            device_id=(me_x, pair, me_y), device_id_type=MESH).start()
 
     @pl.when(on_diagonal)
     def _():

time: 62.3 us -> 62.3 us (level)
  no operation moved by 1% of the time
where the time goes in v11:
time: 62.3 us; the launch traced here: 62 us
  Pallas kernels  50.5 us (81%)
  matrix products  5.68 us (9%)
  local copies, waits for them, and re-layouts  5.66 us (9%)
    pallas_call x1, Pallas kernels, gather_rows(): pl.pallas_call(functools.partial(gather_kernel, n_x, n_z, stride), out_sh...  50.5 us
    dot_general x1, matrix products, per_device(): lax.dot_general(selected, train_grads, (((1,), (1,)), ((), ())), preferre...  4.6 us
    reshape x1, local copies, waits for them, and re-layouts, per_device(): held = held.reshape(n_x, 2, n_zc // 2, rows, width // 128, 128)  1.83 us
    reshape x1, local copies, waits for them, and re-layouts, per_device(): jnp.transpose(held, (2, 1, 3, 0, 4, 5)).reshape(per_col, n_x * width)  1.62 us
    unnamed x4, local copies, waits for them, and re-layouts  1.6 us

profile of v11, /device:TPU:1, one launch (start us, length us, event | category | flops | bytes accessed | tf_op | source)
XLA Modules:
  0.0 62.0 jit_solution(13041331931769730084)
XLA Ops:
  0.0 0.0 copy-start
  0.0 1.6 %copy-done = bf16[2048,512]{1,0:T(8,128)(2,1)S(1)} copy-done((bf16[2048,512]{1,0:T(8,128)(2,1)S(1)}, bf16[2048,512]{1,0:T(8,128)(2,1)}, u32[]{:S(2)}) %copy-start) | copy-done | bytes 2097176
  1.6 1.1 %convolution_convert_fusion = bf16[4,512]{1,0:T(4,128)(2,1)S(1)} fusion(bf16[4,2048]{1,0:T(4,128)(2,1)} %param.5, bf16[2048,512]{1,0:T(8,128)(2,1)S(1)} %copy-done), kind=kOutput, calls=%fused_computation.2 | convolution fusion | flops 8390656 | bytes 2117632 | tf_op jit(solution)/shard_map/dot_general | solution.py:187
  2.7 0.6 reshape.12.block_ref
  3.3 50.5 %shard_map.55 = (bf16[4,2,32,16,128]{4,3,2,1,0:T(8,128)(2,1)}, f32[256,1]{1,0:T(8,128)}) custom-call(bf16[16,128]{1,0:T(8,128)(2,1)} %reshape.12.block_ref, s32[1024,128]{1,0:T(8,128)} %cand_ref.1, s32[2,128]{1,0:T(2,128)} %bitcast.11), custom_call_target="tpu_custom_call" | custom-call | bytes 2097152 | tf_op jit(solution)/shard_map/pallas_call | solution.py:156
  53.8 0.0 copy-start.1
  53.8 1.8 %copy.8 = bf16[4,2,32,4,4,128]{5,4,0,3,1,2:T(4,128)(2,1)S(1)} copy(bf16[4,2,32,4,4,128]{5,4,3,2,1,0:T(4,128)(2,1)} %bitcast.10) | data formatting | bytes 2097152 | tf_op jit(solution)/shard_map/reshape | solution.py:191
  55.7 1.6 %reshape.15 = bf16[256,2048]{1,0:T(8,128)(2,1)} reshape(bf16[32,2,4,4,4,128]{5,4,3,2,1,0:T(4,128)(2,1)S(1)} %bitcast.9) | data formatting | bytes 2097152 | tf_op jit(solution)/shard_map/reshape | solution.py:192
  57.3 0.0 copy-done.1
  57.3 0.1 reduce
  57.4 4.6 %fusion = bf16[256,1024]{1,0:T(8,128)(2,1)} fusion(bf16[256,2048]{1,0:T(8,128)(2,1)} %reshape.15, bf16[1024,2048]{1,0:T(8,128)(2,1)} %param.7, f32[256]{0:T(256)S(1)} %reduce), kind=kOutput, calls=%fused_computation.1 | convolution fusion | flops 1074266112 | bytes 5768192 | tf_op jit(solution)/shard_map/dot_general | solution.py:193
Async XLA Ops:
  0.0 1.6 %copy-start = (bf16[2048,512]{1,0:T(8,128)(2,1)S(1)}, bf16[2048,512]{1,0:T(8,128)(2,1)}, u32[]{:S(2)}) copy-start(bf16[2048,512]{1,0:T(8,128)(2,1)} %param.6) | copy-start | bytes 6291460
  53.8 3.5 %copy-start.1 = (f32[256,1]{1,0:T(8,128)S(1)}, f32[256,1]{1,0:T(8,128)}, u32[]{:S(2)}) copy-start(f32[256,1]{1,0:T(8,128)} %get-tuple-element.8) | copy-start | bytes 3076
